TPU v7x, 128 devices: a whole 4x4x4 slice. The times are simulated.
128 devices in a mesh: dom: 32 (over z, x, core), dp: 4 (over y).
Axes of the slice: x: 4, y: 4, z: 4, core: 2. Of those that a mesh axis runs over, the one named last changes fastest.
Arguments:
- node_latents: bfloat16 [131072, 128], P(('dom', 'dp')), may hold values from -6 to 6
- mesh_latents: bfloat16 [393216, 128], P(('dom', 'dp')), may hold values from -6 to 6
- world_latents: bfloat16 [65536, 128], P(('dom', 'dp')), may hold values from -6 to 6
- mesh_src: int32 [393216], P(('dom', 'dp')), may hold values from 0 to 1535, as said below
- mesh_dst: int32 [393216], P(('dom', 'dp')), may hold values from 0 to 1023
- world_src: int32 [65536], P(('dom', 'dp')), may hold values from 0 to 8191, as said below
- world_dst: int32 [65536], P(('dom', 'dp')), may hold values from 0 to 1023
- send_blocks: int32 [128, 32, 16], P(('dom', 'dp')), may hold values from 0 to 63
- world_count: int32 [128], P(('dom', 'dp')), may hold values from 256 to 512, as said below
- node_cot: bfloat16 [131072, 128], P(('dom', 'dp')), may hold values from -6 to 6
- mesh_cot: bfloat16 [393216, 128], P(('dom', 'dp')), may hold values from -6 to 6
- world_cot: bfloat16 [65536, 128], P(('dom', 'dp')), may hold values from -6 to 6
- first_weights: bfloat16 [3, 384, 128], replicated, may hold values from -0.3125 to 0.3125
- rest_weights: bfloat16 [3, 2, 128, 128], replicated, may hold values from -0.5 to 0.5
- biases: float32 [3, 4, 128], replicated, may hold values from -2 to 2
- gains: float32 [3, 128], replicated, may hold values from 0.1 to 1.9
Outputs:
- new_nodes: bfloat16 [131072, 128], P(('dom', 'dp'))
- new_mesh: bfloat16 [393216, 128], P(('dom', 'dp'))
- new_world: bfloat16 [65536, 128], P(('dom', 'dp'))
- grad_nodes: bfloat16 [131072, 128], P(('dom', 'dp'))
- grad_mesh: bfloat16 [393216, 128], P(('dom', 'dp'))
- grad_world: bfloat16 [65536, 128], P(('dom', 'dp'))
- grad_first: float32 [3, 384, 128], replicated
- grad_rest: float32 [3, 2, 128, 128], replicated
- grad_biases: float32 [3, 4, 128], replicated
- grad_gains: float32 [3, 128], replicated
Inputs may be any that keep to these rules, and one draw needn't show every extreme that they name: `mesh_src`: indexes the 256 rows before a partition's nodes (the last rows of the previous domain of its mesh), its 1024 nodes, then the 256 rows after (the first rows of the next domain); the first domain reads no rows before and the last none after. `world_src`: row j of slot t of the blocks sent by domain p of the same mesh is (p * 16 + t) * 16 + j; a partition reads some slots of each domain, all 16 for at least one. send_blocks[k, p, t] is the block of 16 node rows of partition k put in slot t for domain p of its mesh. Rows of partition k at or past world_count[k] are padding; some partition has all 512 rows live.
All inputs are finite; a program needn't handle non-finite values.
Results may differ from a plain program's by a relative error of at most 0.007.
Values may be sent and summed in bfloat16 or wider, within the bound.
A program may use at most 128 MiB of HBM per device.

v0:
```python
import jax
import jax.numpy as jnp
from jax import lax
from jax.sharding import PartitionSpec as P

HALO = 256
BLK = 16


norm_eps = 1e-05


def extended(value, sides, width):
    for axis, dim in sides:
        devices, length = (lax.axis_size(axis), value.shape[dim])
        up = [(i, (i + 1) % devices) for i in range(devices - 1)]
        down = [(j, i) for i, j in up]
        last = lax.slice_in_dim(value, length - width, length, axis=dim)
        leading = lax.slice_in_dim(value, 0, width, axis=dim)
        before = lax.ppermute(last, axis, up)
        after = lax.ppermute(leading, axis, down)
        value = jnp.concatenate([before, value, after], axis=dim)
    return value


def from_behind(value, axis, steps):
    count = lax.axis_size(axis)
    leading, last = (max(0, -steps), min(count, count - steps))
    return lax.ppermute(value, axis, [(source, source + steps) for source in range(leading, last)])


def matmul(left, right):
    return jnp.dot(left, right, preferred_element_type=jnp.float32)


def matmul_nt(left, right):
    return lax.dot_general(
        left, right, (((1,), (1,)), ((), ())), preferred_element_type=jnp.float32
    )


def matmul_tn(left, right):
    return lax.dot_general(
        left, right, (((0,), (0,)), ((), ())), preferred_element_type=jnp.float32
    )


def silu_grad(values):
    sigma = jax.nn.sigmoid(values)
    return sigma * (1.0 + values * (1.0 - sigma))


def mlp_parts(inputs, first_w, rest_w, bias_rows, gain_row):
    pre_one = matmul(inputs, first_w) + bias_rows[0]
    act_one = jax.nn.silu(pre_one).astype(jnp.bfloat16)
    pre_two = matmul(act_one, rest_w[0]) + bias_rows[1]
    act_two = jax.nn.silu(pre_two).astype(jnp.bfloat16)
    pre_three = matmul(act_two, rest_w[1]) + bias_rows[2]
    centred = pre_three - jnp.mean(pre_three, axis=-1, keepdims=True)
    inv_std = lax.rsqrt(jnp.mean(centred * centred, axis=-1, keepdims=True) + norm_eps)
    normed = centred * inv_std
    output = normed * gain_row + bias_rows[3]
    return (output, (pre_one, act_one, pre_two, act_two, normed, inv_std))


def mlp_backward(inputs, first_w, rest_w, bias_rows, gain_row, cotangent):
    _, saved = mlp_parts(inputs, first_w, rest_w, bias_rows, gain_row)
    pre_one, act_one, pre_two, act_two, normed, inv_std = saved
    grad_gain = jnp.sum(cotangent * normed, axis=0)
    grad_shift = jnp.sum(cotangent, axis=0)
    scaled = cotangent * gain_row
    d_three = inv_std * (
        scaled
        - jnp.mean(scaled, axis=-1, keepdims=True)
        - normed * jnp.mean(scaled * normed, axis=-1, keepdims=True)
    )
    d_three_b = d_three.astype(jnp.bfloat16)
    grad_w3 = matmul_tn(act_two, d_three_b)
    d_two = matmul_nt(d_three_b, rest_w[1]) * silu_grad(pre_two)
    d_two_b = d_two.astype(jnp.bfloat16)
    grad_w2 = matmul_tn(act_one, d_two_b)
    d_one = matmul_nt(d_two_b, rest_w[0]) * silu_grad(pre_one)
    d_one_b = d_one.astype(jnp.bfloat16)
    grad_w1 = matmul_tn(inputs, d_one_b)
    grad_in = matmul_nt(d_one_b, first_w)
    bias_grads = jnp.stack(
        [jnp.sum(d_one, axis=0), jnp.sum(d_two, axis=0), jnp.sum(d_three, axis=0), grad_shift]
    )
    return (grad_in, (grad_w1, jnp.stack([grad_w2, grad_w3]), bias_grads, grad_gain))


def per_device(
    node_latents,
    mesh_latents,
    world_latents,
    mesh_src,
    mesh_dst,
    world_src,
    world_dst,
    send_blocks,
    world_count,
    node_cot,
    mesh_cot,
    world_cot,
    first_weights,
    rest_weights,
    biases,
    gains,
):
    node_count = node_latents.shape[0]
    latent_width = node_latents.shape[1]
    weights = [
        (first_weights[which], rest_weights[which], biases[which], gains[which])
        for which in range(3)
    ]
    padded = extended(node_latents, (("dom", 0),), HALO)
    send_index = (send_blocks[0][:, :, None] * BLK + jnp.arange(BLK, dtype=jnp.int32)).reshape(-1)
    incoming = lax.all_to_all(
        node_latents[send_index], "dom", split_axis=0, concat_axis=0, tiled=True
    )
    recv_rows = incoming.shape[0]
    mesh_inputs = jnp.concatenate([mesh_latents, padded[mesh_src], node_latents[mesh_dst]], axis=1)
    mesh_message, _ = mlp_parts(mesh_inputs, *weights[0])
    new_mesh = (mesh_latents.astype(jnp.float32) + mesh_message).astype(jnp.bfloat16)
    mesh_total = jax.ops.segment_sum(mesh_message, mesh_dst, num_segments=node_count)
    world_total_rows = world_latents.shape[0]
    live_rows = world_count[0]

    def world_inputs(row_count):
        keep_rows = (jnp.arange(row_count, dtype=jnp.int32) < live_rows).astype(jnp.float32)[
            :, None
        ]
        inputs = jnp.concatenate(
            [world_latents, incoming[world_src], node_latents[world_dst]], axis=1
        )
        return (world_latents, world_src, world_dst, keep_rows, inputs)

    latents, sources, targets, keep_rows, inputs = world_inputs(world_total_rows)
    message = mlp_parts(inputs, *weights[1])[0] * keep_rows
    updated = (latents.astype(jnp.float32) + message).astype(jnp.bfloat16)
    world_total = jax.ops.segment_sum(message, targets, num_segments=node_count)
    node_input = jnp.concatenate(
        [node_latents, mesh_total.astype(jnp.bfloat16), world_total.astype(jnp.bfloat16)], axis=1
    )
    node_update, _ = mlp_parts(node_input, *weights[2])
    new_nodes = (node_latents.astype(jnp.float32) + node_update).astype(jnp.bfloat16)
    node_back, node_grads = mlp_backward(node_input, *weights[2], node_cot.astype(jnp.float32))
    grad_local = node_cot.astype(jnp.float32) + node_back[:, :latent_width]
    mesh_back = node_back[:, latent_width : 2 * latent_width]
    world_back = node_back[:, 2 * latent_width :]
    mesh_upstream = mesh_cot.astype(jnp.float32) + mesh_back[mesh_dst]
    mesh_in_grad, mesh_grads = mlp_backward(mesh_inputs, *weights[0], mesh_upstream)
    grad_mesh = (mesh_cot.astype(jnp.float32) + mesh_in_grad[:, :latent_width]).astype(jnp.bfloat16)
    padded_grad = jax.ops.segment_sum(
        mesh_in_grad[:, latent_width : 2 * latent_width],
        mesh_src,
        num_segments=node_count + 2 * HALO,
    )
    from_right = from_behind(padded_grad[:HALO].astype(jnp.bfloat16), "dom", -1).astype(jnp.float32)
    from_left = from_behind(padded_grad[HALO + node_count :].astype(jnp.bfloat16), "dom", 1).astype(
        jnp.float32
    )
    grad_local = grad_local + padded_grad[HALO : HALO + node_count]
    grad_local = grad_local + jax.ops.segment_sum(
        mesh_in_grad[:, 2 * latent_width :], mesh_dst, num_segments=node_count
    )
    grad_local = grad_local + jnp.pad(from_left, ((0, node_count - HALO), (0, 0)))
    grad_local = grad_local + jnp.pad(from_right, ((node_count - HALO, 0), (0, 0)))
    latents, sources, targets, keep_rows, inputs = world_inputs(world_total_rows)
    cotangent = world_cot.astype(jnp.float32)
    in_grad, weight_grads = mlp_backward(
        inputs, *weights[1], keep_rows * (cotangent + world_back[targets])
    )
    own_grad = (cotangent + in_grad[:, :latent_width]).astype(jnp.bfloat16)
    to_source = jax.ops.segment_sum(
        in_grad[:, latent_width : 2 * latent_width], sources, num_segments=recv_rows
    )
    to_target = jax.ops.segment_sum(
        in_grad[:, 2 * latent_width :], targets, num_segments=node_count
    )
    returned = lax.all_to_all(
        to_source.astype(jnp.bfloat16), "dom", split_axis=0, concat_axis=0, tiled=True
    ).astype(to_source.dtype)
    grad_local = (
        grad_local + to_target + jax.ops.segment_sum(returned, send_index, num_segments=node_count)
    )
    grad_nodes = grad_local.astype(jnp.bfloat16)
    divisor = lax.axis_size("dom") * lax.axis_size("dp")
    summed_all = lax.psum(
        (
            jnp.stack([mesh_grads[0], weight_grads[0], node_grads[0]]),
            jnp.stack([mesh_grads[1], weight_grads[1], node_grads[1]]),
            jnp.stack([mesh_grads[2], weight_grads[2], node_grads[2]]),
            jnp.stack([mesh_grads[3], weight_grads[3], node_grads[3]]),
        ),
        ("dom", "dp"),
    )
    return (
        new_nodes,
        new_mesh,
        updated,
        grad_nodes,
        grad_mesh,
        own_grad,
        summed_all[0] / divisor,
        summed_all[1] / divisor,
        summed_all[2] / divisor,
        summed_all[3] / divisor,
    )


def solution(mesh):
    return jax.shard_map(
        per_device,
        mesh=mesh,
        in_specs=(
            P(("dom", "dp"), None),
            P(("dom", "dp"), None),
            P(("dom", "dp"), None),
            P(("dom", "dp")),
            P(("dom", "dp")),
            P(("dom", "dp")),
            P(("dom", "dp")),
            P(("dom", "dp"), None, None),
            P(("dom", "dp")),
            P(("dom", "dp"), None),
            P(("dom", "dp"), None),
            P(("dom", "dp"), None),
            P(),
            P(),
            P(),
            P(),
        ),
        out_specs=(
            P(("dom", "dp"), None),
            P(("dom", "dp"), None),
            P(("dom", "dp"), None),
            P(("dom", "dp"), None),
            P(("dom", "dp"), None),
            P(("dom", "dp"), None),
            P(),
            P(),
            P(),
            P(),
        ),
        check_vma=False,
    )
```

profile of v0, /device:TPU:1, one launch (start us, length us, event | category | flops | bytes accessed | tf_op | source)
XLA Modules:
  0.0 446.7 jit_solution(10233269312754770029)
XLA Ops:
  7.2 1.6 fusion.101
  8.8 4.5 %collective-permute-start = (bf16[256,128]{1,0:T(8,128)(2,1)}, bf16[256,128]{1,0:T(8,128)(2,1)}, u32[]{:S(2)}, u32[]{:S(2)}) collective-permute-start(bf16[256,128]{1,0:T(8,128)(2,1)} %get-tuple-element.63), channel_id=1, source_target_pairs={{0,4},{4,8},{8,12},{12,16},{16,20},{20,24},{24,28},{28,32},{32,36}... | collective-permute-start | bytes 196616 | tf_op jit(solution)/shard_map/ppermute | solution.py:20
  13.3 1.9 collective-permute-start.1
  16.3 29.5 %gather_fusion.2 = bf16[8192,128]{1,0:T(8,128)(2,1)} fusion(bf16[1024,128]{1,0:T(8,128)(2,1)S(1)} %copy-done, s32[8192]{0:T(1024)S(1)} %broadcast_clamp_fusion), kind=kCustom, calls=%fused_computation.2 | custom fusion | bytes 4227072 | tf_op jit(solution)/shard_map/gather | solution.py:119
  45.8 8.7 %all-to-all-start = ((bf16[32,256,128]{2,1,0:T(8,128)(2,1)}), bf16[32,256,128]{2,1,0:T(8,128)(2,1)}, u32[]{:S(2)}, u32[]{:S(2)}) async-start(bf16[32,256,128]{2,1,0:T(8,128)(2,1)} %bitcast.10), calls=%async_computation | async-start | bytes 4194304 | tf_op jit(solution)/shard_map/all_to_all | solution.py:118
  62.1 1.9 gather_fusion.4
  64.2 2.3 copy.56
  66.6 11.5 %gather_fusion.1 = bf16[3072,128]{1,0:T(8,128)(2,1)} fusion(bf16[1024,128]{1,0:T(8,128)(2,1)S(1)} %copy-done, s32[3072]{0:T(1024)S(1)} %get-tuple-element.99), kind=kCustom, calls=%fused_computation.1 | custom fusion | bytes 1585152 | tf_op jit(solution)/shard_map/gather | solution.py:122
  79.0 11.5 %gather_fusion = bf16[3072,128]{1,0:T(8,128)(2,1)} fusion(bf16[1536,128]{1,0:T(8,128)(2,1)S(1)} %pad_maximum_fusion.2, s32[3072]{0:T(1024)S(1)} %get-tuple-element.98), kind=kCustom, calls=%fused_computation | custom fusion | bytes 1585152 | tf_op jit(solution)/shard_map/gather | solution.py:122
  90.5 1.4 constant_dynamic-update-slice_fusion.1
  92.2 1.8 convolution_add_fusion.2
  95.4 1.5 fusion.103
  98.0 1.6 add_convert_fusion
  100.8 3.1 copy.49
  103.9 17.6 %scatter_custom_fusion = f32[1024,128]{1,0:T(8,128)S(1)} fusion(s32[3072]{0:T(1024)} %param.20, f32[3072,128]{1,0:T(8,128)} %copy.49, f32[]{:T(128)} %constant.60.clone.1), kind=kCustom, calls=%fused_computation.116 | custom fusion | flops 393216 | bytes 524800 | tf_op jit(solution)/shard_map/scatter-add | solution.py:125
  122.2 3.1 gather_fusion.3
  129.8 2.5 scatter_custom_fusion.1
  132.4 1.4 convolution_add_fusion.5
  143.6 1.5 multiply_reduce_fusion.5
  145.1 1.5 fusion.97
  147.5 1.6 fusion.107
  150.0 1.6 fusion.108
  153.7 3.4 scatter_custom_fusion.4
  157.1 10.9 %gather_fusion.5 = f32[3072,128]{1,0:T(8,128)} fusion(f32[1024,128]{1,0:T(8,128)S(1)} %get-tuple-element.57, s32[3072]{0:T(1024)S(1)} %copy-done.35), kind=kCustom, calls=%fused_computation.5 | custom fusion | bytes 3158016 | tf_op jit(solution)/shard_map/gather | solution.py:151
  168.0 3.1 copy.57
  171.2 3.7 multiply_reduce_fusion
  174.9 1.4 fusion.96
  177.6 2.2 fusion.109
  181.0 2.9 fusion.110
  183.9 5.0 %scatter_custom_fusion.5 = f32[8192,128]{1,0:T(8,128)} fusion(s32[512]{0:T(512)} %param.21, f32[]{:T(128)} %constant.60.clone.1, f32[512,384]{1,0:T(8,128)} %copy-done.11), kind=kCustom, calls=%fused_computation.21 | custom fusion | flops 65536 | bytes 4456960 | tf_op jit(solution)/shard_map/scatter-add | solution.py:175
  188.9 2.7 convolution_bitcast_fusion.2
  191.6 3.8 fusion.20
  195.4 16.6 %scatter_custom_fusion.2 = f32[1536,128]{1,0:T(8,128)} fusion(s32[3072]{0:T(1024)} %param.19, f32[3072,384]{1,0:T(8,128)} %fusion.20, f32[]{:T(128)} %constant.60.clone.1), kind=kCustom, calls=%fused_computation.28 | custom fusion | flops 393216 | bytes 2359808 | tf_op jit(solution)/shard_map/scatter-add | solution.py:154
  215.7 3.7 convert_element_type.147
  219.4 7.4 %all-to-all-start.1 = ((bf16[32,256,128]{2,1,0:T(8,128)(2,1)}), bf16[32,256,128]{2,1,0:T(8,128)(2,1)}, u32[]{:S(2)}, u32[]{:S(2)}) async-start(bf16[32,256,128]{2,1,0:T(8,128)(2,1)} %bitcast.29), calls=%async_computation.1 | async-start | bytes 4194304 | tf_op jit(solution)/shard_map/all_to_all | solution.py:181
  226.9 1.5 copy.58
  229.1 3.5 collective-permute-start.2
  232.7 1.9 collective-permute-start.3
  234.6 1.7 copy.71
  236.3 1.6 fusion.4
  242.1 8.6 %collective-permute-done.2 = bf16[256,128]{0,1:T(8,128)(2,1)S(1)} collective-permute-done((bf16[256,128]{0,1:T(8,128)(2,1)}, bf16[256,128]{0,1:T(8,128)(2,1)S(1)}, u32[]{:S(2)}, u32[]{:S(2)}) %collective-permute-start.2) | collective-permute-done | bytes 65568 | tf_op jit(solution)/shard_map/ppermute | solution.py:29
  250.7 1.9 collective-permute-done.3
  254.3 17.6 %scatter_custom_fusion.3 = f32[1024,128]{1,0:T(8,128)S(1)} fusion(f32[1024,128]{1,0:T(8,128)S(1)} %copy.60, s32[3072]{0:T(1024)} %param.20, f32[3072,384]{1,0:T(8,128)} %fusion.20), kind=kCustom, calls=%fused_computation.26 | custom fusion | flops 393216 | bytes 2097152 | tf_op jit(solution)/shard_map/scatter-add | solution.py:164
  271.9 67.1 %all-reduce.2 = (f32[3,4,128]{2,1,0:T(4,128)S(1)}, f32[3,128]{1,0:T(4,128)S(1)}) all-reduce(f32[3,4,128]{2,1,0:T(4,128)S(1)} %pad_maximum_fusion.6, f32[3,128]{1,0:T(4,128)S(1)} %pad_maximum_fusion.7), channel_id=1, replica_groups=mesh['dom'=32,'dp'=4] {'dom','dp'}, use_global_device_ids=true, to_apply=%region_33.34 | all-reduce | flops 1920 | bytes 15360 | tf_op jit(solution)/shard_map/psum | solution.py:189
  340.2 50.0 %all-reduce.6.cloned.1.call-done = (f32[3,384,128]{2,1,0:T(8,128)}, f32[3,2,128,128]{3,2,1,0:T(8,128)}) async-done(((f32[3,384,128]{2,1,0:T(8,128)}, f32[3,2,128,128]{3,2,1,0:T(8,128)}), (f32[3,384,128]{2,1,0:T(8,128)}, f32[3,2,128,128]{3,2,1,0:T(8,128)})) %all-reduce.6.cloned.1.call-update) | async-done | bytes 983056 | tf_op jit(solution)/shard_map/psum | solution.py:189
  390.2 1.8 broadcast_multiply_fusion.1
  392.0 1.9 broadcast_multiply_fusion
  393.9 44.8 %scatter_custom_fusion.6 = f32[1024,128]{1,0:T(8,128)S(1)} fusion(f32[1024,128]{1,0:T(8,128)S(1)} %add.433, s32[8192]{0:T(1024)} %reshape.285, bf16[8192,128]{1,0:T(8,128)(2,1)} %bitcast.61), kind=kCustom, calls=%fused_computation.14 | custom fusion | flops 2097152 | bytes 2621440 | tf_op jit(solution)/shard_map/scatter-add | solution.py:185
  (278 shorter events, 45.8 us)
Async XLA Ops:
  7.2 9.2 %copy-start = (bf16[1024,128]{1,0:T(8,128)(2,1)S(1)}, bf16[1024,128]{1,0:T(8,128)(2,1)}, u32[]{:S(2)}) copy-start(bf16[1024,128]{1,0:T(8,128)(2,1)} %param.16) | copy-start | bytes 786436
  8.8 69.3 %collective-permute-start = (bf16[256,128]{1,0:T(8,128)(2,1)}, bf16[256,128]{1,0:T(8,128)(2,1)}, u32[]{:S(2)}, u32[]{:S(2)}) collective-permute-start(bf16[256,128]{1,0:T(8,128)(2,1)} %get-tuple-element.63), channel_id=1, source_target_pairs={{0,4},{4,8},{8,12},{12,16},{16,20},{20,24},{24,28},{28,32},{32,36}... | collective-permute-start | bytes 196616 | tf_op jit(solution)/shard_map/ppermute | solution.py:20
  13.3 64.8 %collective-permute-start.1 = (bf16[256,128]{1,0:T(8,128)(2,1)}, bf16[256,128]{1,0:T(8,128)(2,1)}, u32[]{:S(2)}, u32[]{:S(2)}) collective-permute-start(bf16[256,128]{1,0:T(8,128)(2,1)} %get-tuple-element.64), channel_id=1, source_target_pairs={{4,0},{8,4},{12,8},{16,12},{20,16},{24,20},{28,24},{32,28},{36,32}... | collective-permute-start | bytes 196616 | tf_op jit(solution)/shard_map/ppermute | solution.py:21
  45.8 10.4 %copy-start.25 = (bf16[512,128]{1,0:T(8,128)(2,1)S(1)}, bf16[512,128]{1,0:T(8,128)(2,1)}, u32[]{:S(2)}) copy-start(bf16[512,128]{1,0:T(8,128)(2,1)} %param.18) | copy-start | bytes 393220
  45.8 76.4 %all-to-all-start = ((bf16[32,256,128]{2,1,0:T(8,128)(2,1)}), bf16[32,256,128]{2,1,0:T(8,128)(2,1)}, u32[]{:S(2)}, u32[]{:S(2)}) async-start(bf16[32,256,128]{2,1,0:T(8,128)(2,1)} %bitcast.10), calls=%async_computation | async-start | bytes 4194304 | tf_op jit(solution)/shard_map/all_to_all | solution.py:118
  57.0 3.2 copy-start.70
  57.0 3.8 copy-start.66
  57.0 3.8 copy-start.65
  57.0 3.8 copy-start.55
  57.0 4.4 copy-start.33
  58.2 5.9 %copy-start.27 = (bf16[1024,128]{1,0:T(8,128)(2,1)S(1)}, bf16[1024,128]{1,0:T(8,128)(2,1)}, u32[]{:S(2)}) copy-start(bf16[1024,128]{1,0:T(8,128)(2,1)} %param.25) | copy-start | bytes 786436
  62.1 4.4 copy-start.49
  62.1 4.4 copy-start.50
  62.1 4.4 copy-start.51
  66.5 11.5 %copy-start.34 = (s32[3072]{0:T(1024)}, s32[3072]{0:T(1024)S(1)}, u32[]{:S(2)}) copy-start(s32[3072]{0:T(1024)S(1)} %get-tuple-element.99) | copy-start | bytes 36868
  78.1 50.8 %copy-start.44 = (f32[512]{0:T(512)}, f32[512]{0:T(512)S(1)}, u32[]{:S(2)}) copy-start(f32[512]{0:T(512)S(1)} %fusion.89) | copy-start | bytes 6148
  103.8 21.4 %copy-start.14 = (bf16[512,384]{1,0:T(8,128)(2,1)S(1)}, bf16[512,384]{1,0:T(8,128)(2,1)}, u32[]{:S(2)}) copy-start(bf16[512,384]{1,0:T(8,128)(2,1)} %constant_dynamic-update-slice_fusion.5) | copy-start | bytes 1179652
  103.8 21.5 %copy-start.24 = (bf16[512,128]{1,0:T(8,128)(2,1)S(1)}, bf16[512,128]{1,0:T(8,128)(2,1)}, u32[]{:S(2)}) copy-start(bf16[512,128]{1,0:T(8,128)(2,1)} %gather_fusion.4) | copy-start | bytes 393220
  122.2 4.5 %copy-start.74 = (f32[128]{0:T(128)S(1)}, f32[128]{0:T(128)}, u32[]{:S(2)}) copy-start(f32[128]{0:T(128)} %get-tuple-element.70) | copy-start | bytes 1540
  122.2 5.5 %copy-start.73 = (f32[128]{0:T(128)S(1)}, f32[128]{0:T(128)}, u32[]{:S(2)}) copy-start(f32[128]{0:T(128)} %get-tuple-element.69) | copy-start | bytes 1540
  125.4 3.4 copy-start.15
  151.6 5.5 %copy-start.35 = (s32[3072]{0:T(1024)S(1)}, s32[3072]{0:T(1024)}, u32[]{:S(2)}) copy-start(s32[3072]{0:T(1024)} %copy-done.34) | copy-start | bytes 36868
  153.7 3.4 copy-start.11
  168.0 3.1 copy-start.32
  168.0 3.1 copy-start.54
  171.2 3.7 copy-start.3
  183.9 5.0 %copy-start.2 = (bf16[3072,384]{1,0:T(8,128)(2,1)S(1)}, bf16[3072,384]{1,0:T(8,128)(2,1)}, u32[]{:S(2)}) copy-start(bf16[3072,384]{1,0:T(8,128)(2,1)} %copy-done.1) | copy-start | bytes 7077892
  219.4 174.5 %all-to-all-start.1 = ((bf16[32,256,128]{2,1,0:T(8,128)(2,1)}), bf16[32,256,128]{2,1,0:T(8,128)(2,1)}, u32[]{:S(2)}, u32[]{:S(2)}) async-start(bf16[32,256,128]{2,1,0:T(8,128)(2,1)} %bitcast.29), calls=%async_computation.1 | async-start | bytes 4194304 | tf_op jit(solution)/shard_map/all_to_all | solution.py:181
  226.9 7.7 %slice-start = ((f32[3072,384]{1,0:T(8,128)}), f32[3072,128]{1,0:T(8,128)S(1)}, s32[]{:S(2)}) async-start(f32[3072,384]{1,0:T(8,128)} %fusion.20), calls=%async_computation.3 | async-start | bytes 3145728 | tf_op jit(solution)/shard_map/slice | solution.py:153
  226.9 163.3 %all-reduce.6.cloned.1.call-start = ((), (), s32[]{:S(2)}) async-start(), calls=%async_computation.2 | async-start | bytes 1966080 | tf_op jit(solution)/shard_map/psum | solution.py:189
  229.1 21.6 %collective-permute-start.2 = (bf16[256,128]{0,1:T(8,128)(2,1)}, bf16[256,128]{0,1:T(8,128)(2,1)S(1)}, u32[]{:S(2)}, u32[]{:S(2)}) collective-permute-start(bf16[256,128]{0,1:T(8,128)(2,1)} %get-tuple-element.60), channel_id=1, source_target_pairs={{0,4},{4,8},{8,12},{12,16},{16,20},{20,24},{24,28},{28,32},{32,36}... | collective-permute-start | bytes 196616 | tf_op jit(solution)/shard_map/ppermute | solution.py:29
  232.7 20.0 %collective-permute-start.3 = (bf16[256,128]{0,1:T(8,128)(2,1)}, bf16[256,128]{0,1:T(8,128)(2,1)S(1)}, u32[]{:S(2)}, u32[]{:S(2)}) collective-permute-start(bf16[256,128]{0,1:T(8,128)(2,1)} %get-tuple-element.61), channel_id=1, source_target_pairs={{4,0},{8,4},{12,8},{16,12},{20,16},{24,20},{28,24},{32,28},{36,32}... | collective-permute-start | bytes 196616 | tf_op jit(solution)/shard_map/ppermute | solution.py:29
  237.9 3.2 copy-start.21
  237.9 3.2 copy-start.22
  237.9 3.1 copy-start.30
  239.2 13.4 %copy-start.7 = (f32[1024,128]{0,1:T(8,128)S(1)}, f32[1024,128]{0,1:T(8,128)}, u32[]{:S(2)}) copy-start(f32[1024,128]{0,1:T(8,128)} %copy-done.6) | copy-start | bytes 1572868
  239.2 13.4 %copy-start.18 = (f32[1024,128]{0,1:T(8,128)S(1)}, f32[1024,128]{0,1:T(8,128)}, u32[]{:S(2)}) copy-start(f32[1024,128]{0,1:T(8,128)} %copy.70) | copy-start | bytes 1572868
  239.2 13.4 %copy-start.20 = (bf16[1024,128]{0,1:T(8,128)(2,1)S(1)}, bf16[1024,128]{0,1:T(8,128)(2,1)}, u32[]{:S(2)}) copy-start(bf16[1024,128]{0,1:T(8,128)(2,1)} %copy.48) | copy-start | bytes 786436
  239.2 13.4 %copy-start.42 = (f32[1024]{0:T(1024)S(1)}, f32[1024]{0:T(1024)}, u32[]{:S(2)}) copy-start(f32[1024]{0:T(1024)} %copy-done.41) | copy-start | bytes 12292
  239.3 13.4 %copy-start.46 = (f32[1024]{0:T(1024)S(1)}, f32[1024]{0:T(1024)}, u32[]{:S(2)}) copy-start(f32[1024]{0:T(1024)} %copy-done.45) | copy-start | bytes 12292
  239.3 13.4 %copy-start.48 = (f32[1024]{0:T(1024)S(1)}, f32[1024]{0:T(1024)}, u32[]{:S(2)}) copy-start(f32[1024]{0:T(1024)} %copy-done.47) | copy-start | bytes 12292
  239.3 13.4 %copy-start.57 = (f32[128]{0:T(128)S(1)}, f32[128]{0:T(128)}, u32[]{:S(2)}) copy-start(f32[128]{0:T(128)} %get-tuple-element.77) | copy-start | bytes 1540
  239.3 13.4 %copy-start.59 = (f32[128]{0:T(128)S(1)}, f32[128]{0:T(128)}, u32[]{:S(2)}) copy-start(f32[128]{0:T(128)} %get-tuple-element.65) | copy-start | bytes 1540
  241.9 11.2 %copy-start.77 = (f32[128]{0:T(128)S(1)}, f32[128]{0:T(128)}, u32[]{:S(2)}) copy-start(f32[128]{0:T(128)} %get-tuple-element.86) | copy-start | bytes 1540
  241.9 11.2 %copy-start.78 = (f32[128]{0:T(128)S(1)}, f32[128]{0:T(128)}, u32[]{:S(2)}) copy-start(f32[128]{0:T(128)} %get-tuple-element.88) | copy-start | bytes 1540
  242.0 11.2 %copy-start.60 = (f32[128]{0:T(128)S(1)}, f32[128]{0:T(128)}, u32[]{:S(2)}) copy-start(f32[128]{0:T(128)} %get-tuple-element.36) | copy-start | bytes 1540
  242.0 11.2 %copy-start.61 = (f32[128]{0:T(128)S(1)}, f32[128]{0:T(128)}, u32[]{:S(2)}) copy-start(f32[128]{0:T(128)} %get-tuple-element.30) | copy-start | bytes 1540
  254.1 17.8 %copy-start.17 = (f32[1024,128]{1,0:T(8,128)S(1)}, f32[1024,128]{1,0:T(8,128)}, u32[]{:S(2)}) copy-start(f32[1024,128]{1,0:T(8,128)} %scatter_custom_fusion.4) | copy-start | bytes 1572868
  (49 other events, 89.5 us)
Sparse Core Ops, SparseCore 0:
  242.1 148.0 all-reduce.5
where the time goes:
time: 455 us; the launch traced here: 447 us
  other arithmetic  136 us (30%)
  local copies, waits for them, and re-layouts  101 us (22%)
  blocking collectives  67.1 us (15%)
  waiting for transfers between devices  60.6 us (13%)
  matrix products  37.3 us (8%)
  starting transfers between devices  28.1 us (6%)
  between operations  16.5 us (4%)
    psum x1, blocking collectives, per_device(): lax.psum((jnp.stack([mesh_grads[0], weight_grads[0], node_grads[0]]), jnp...  67.1 us
    psum x1, waiting for transfers between devices, per_device(): lax.psum((jnp.stack([mesh_grads[0], weight_grads[0], node_grads[0]]), jnp...  50 us
    scatter-add x1, other arithmetic, per_device(): jax.ops.segment_sum(returned, send_index, num_segments=node_count)  44.8 us
    gather x1, local copies, waits for them, and re-layouts, per_device(): node_latents[send_index]  29.5 us
    unnamed x194, local copies, waits for them, and re-layouts  18.2 us
    scatter-add x1, other arithmetic, per_device(): jax.ops.segment_sum(mesh_message, mesh_dst, num_segments=node_count)  17.6 us
    scatter-add x1, other arithmetic, per_device(): jax.ops.segment_sum(mesh_in_grad[:, 2 * latent_width:], mesh_dst, num_seg...  17.6 us
    scatter-add x1, other arithmetic, per_device(): jax.ops.segment_sum(mesh_in_grad[:, latent_width:2 * latent_width], mesh_...  16.6 us
  transfers between devices with their start and end apart: 7, of which 3 were waited for; matrix products, arithmetic and copies ran while one was open for 29% of the time, Pallas kernels for 0%

commit v1 on v0

v1 whole, which is shorter than its diff:
```python
import functools

import jax
import jax.numpy as jnp
from jax import lax
from jax.experimental import pallas as pl
from jax.experimental.pallas import tpu as pltpu
from jax.sharding import PartitionSpec as P

D = 128
HALO = 256
BLK = 16
ROWS = 512
EPS = 1e-05
GRADS = 2048
BF = jnp.bfloat16
F32 = jnp.float32
MESH = pl.DeviceIdType.MESH


def nn(left, right):
    return jnp.dot(left, right, preferred_element_type=F32)


def nt(left, right):
    return lax.dot_general(left, right, (((1,), (1,)), ((), ())), preferred_element_type=F32)


def tn(left, right):
    return lax.dot_general(left, right, (((0,), (0,)), ((), ())), preferred_element_type=F32)


def sigma(values):
    return 0.5 + 0.5 * jnp.tanh(0.5 * values)


def lane_mean(values):
    return jnp.sum(values, axis=-1, keepdims=True) * (1.0 / D)


def pick_rows(out_ref, index_ref, first, groups, blocks):
    lane = lax.broadcasted_iota(jnp.int32, (128, 128), 1)
    for g in range(groups):
        row = index_ref[pl.ds(first + g, 1), :]
        column = jnp.transpose(jnp.broadcast_to(row, (128, 128)))
        if blocks <= 16:
            for b in range(blocks):
                hit = column == lane + b * 128
                out_ref[g * 128 : (g + 1) * 128, b * 128 : (b + 1) * 128] = jnp.where(
                    hit, 1.0, 0.0
                ).astype(BF)
        else:

            @pl.loop(0, blocks)
            def _(b):
                hit = column == lane + b * 128
                out_ref[g * 128 : (g + 1) * 128, pl.ds(pl.multiple_of(b * 128, 128), 128)] = (
                    jnp.where(hit, 1.0, 0.0).astype(BF)
                )


def pick_columns(out_ref, index_ref, first, groups, blocks):
    down = lax.broadcasted_iota(jnp.int32, (128, 128), 0)
    for g in range(groups):
        row = jnp.broadcast_to(index_ref[pl.ds(first + g, 1), :], (128, 128))
        if blocks <= 16:
            for b in range(blocks):
                hit = row == down + b * 128
                out_ref[b * 128 : (b + 1) * 128, g * 128 : (g + 1) * 128] = jnp.where(
                    hit, 1.0, 0.0
                ).astype(BF)
        else:

            @pl.loop(0, blocks)
            def _(b):
                hit = row == down + b * 128
                out_ref[pl.ds(pl.multiple_of(b * 128, 128), 128), g * 128 : (g + 1) * 128] = (
                    jnp.where(hit, 1.0, 0.0).astype(BF)
                )


def layers(which, pre_one, rest_ref, bias_ref):
    sig_one = sigma(pre_one)
    act_one = (pre_one * sig_one).astype(BF)
    pre_two = nn(act_one, rest_ref[which, 0]) + bias_ref[which, 1:2, :]
    sig_two = sigma(pre_two)
    act_two = (pre_two * sig_two).astype(BF)
    pre_three = nn(act_two, rest_ref[which, 1]) + bias_ref[which, 2:3, :]
    centred = pre_three - lane_mean(pre_three)
    inv_std = lax.rsqrt(lane_mean(centred * centred) + EPS)
    return sig_one, act_one, pre_two, sig_two, act_two, centred, inv_std


def layers_back(which, cot, pre_one, sig_one, pre_two, sig_two, normed, inv_std, rest_ref, gain_ref):
    scaled = cot * gain_ref[which : which + 1, :]
    d_three = inv_std * (scaled - lane_mean(scaled) - normed * lane_mean(scaled * normed))
    d_three_b = d_three.astype(BF)
    d_two = nt(d_three_b, rest_ref[which, 1]) * (sig_two * (1.0 + pre_two * (1.0 - sig_two)))
    d_two_b = d_two.astype(BF)
    d_one = nt(d_two_b, rest_ref[which, 0]) * (sig_one * (1.0 + pre_one * (1.0 - sig_one)))
    d_one_b = d_one.astype(BF)

    def total(values):
        return jnp.sum(values, axis=0, keepdims=True)

    sums = jnp.concatenate(
        [
            total(d_one),
            total(d_two),
            total(d_three),
            total(cot),
            total(cot * normed),
            jnp.zeros((3, D), F32),
        ],
        axis=0,
    )
    return d_one_b, d_two_b, d_three_b, sums


def prep_kernel(blocks_ref, node_ref, out_ref):
    @pl.loop(0, 512, unroll=8)
    def _(i):
        block = blocks_ref[i]
        out_ref[pl.ds(pl.multiple_of(i * BLK, BLK), BLK), :] = node_ref[
            pl.ds(pl.multiple_of(block * BLK, BLK), BLK), :
        ]


def mesh_kernel(
    src_ref, dst_ref, node_ref, before_ref, after_ref, lat_ref, first_ref, rest_ref, bias_ref,
    gain_ref, new_ref, sum_ref, one_ref, two_ref, centred_ref, pick_src, pick_dst, put_dst, total
):
    step = pl.program_id(0)
    groups = ROWS // 128
    first = step * groups
    pick_rows(pick_src, src_ref, first, groups, 12)
    pick_rows(pick_dst, dst_ref, first, groups, 8)
    pick_columns(put_dst, dst_ref, first, groups, 8)
    source = (
        nn(pick_src[:, :HALO], before_ref[...])
        + nn(pick_src[:, HALO : HALO + 1024], node_ref[...])
        + nn(pick_src[:, HALO + 1024 :], after_ref[...])
    ).astype(BF)
    target = nn(pick_dst[...], node_ref[...]).astype(BF)
    lat = lat_ref[...]
    pre_one = (
        nn(lat, first_ref[0, :D, :])
        + nn(source, first_ref[0, D : 2 * D, :])
        + nn(target, first_ref[0, 2 * D :, :])
        + bias_ref[0, 0:1, :]
    )
    _, _, pre_two, _, _, centred, inv_std = layers(0, pre_one, rest_ref, bias_ref)
    message = centred * inv_std * gain_ref[0:1, :] + bias_ref[0, 3:4, :]
    new_ref[...] = (lat.astype(F32) + message).astype(BF)
    one_ref[...] = pre_one
    two_ref[...] = pre_two
    centred_ref[...] = centred
    added = nn(put_dst[...], message.astype(BF))

    @pl.when(step == 0)
    def _():
        total[...] = added

    @pl.when(step > 0)
    def _():
        total[...] += added

    @pl.when(step == pl.num_programs(0) - 1)
    def _():
        sum_ref[...] = total[...].astype(BF)


def middle_kernel(
    count_ref, src_ref, dst_ref, node_ref, incoming_ref, lat_ref, cot_ref, sum_ref, node_cot_ref,
    first_ref, rest_ref, bias_ref, gain_ref, new_nodes_ref, new_world_ref, grad_world_ref,
    back_ref, mesh_back_ref, local_ref, world_grad_ref, node_grad_ref, small_ref, pick_src,
    pick_dst, put_src, put_dst, world_back
):
    groups = 4
    live_rows = count_ref[0]
    keep = (lax.broadcasted_iota(jnp.int32, (512, D), 0) < live_rows).astype(F32)
    pick_rows(pick_src, src_ref, 0, groups, 64)
    pick_rows(pick_dst, dst_ref, 0, groups, 8)
    pick_columns(put_dst, dst_ref, 0, groups, 8)
    source = nn(pick_src[...], incoming_ref[...]).astype(BF)
    target = nn(pick_dst[...], node_ref[...]).astype(BF)
    lat = lat_ref[...]
    inputs = jnp.concatenate([lat, source, target], axis=1)
    pre_one = nn(inputs, first_ref[1]) + bias_ref[1, 0:1, :]
    sig_one, act_one, pre_two, sig_two, act_two, centred, inv_std = layers(
        1, pre_one, rest_ref, bias_ref
    )
    normed = centred * inv_std
    message = keep * (normed * gain_ref[1:2, :] + bias_ref[1, 3:4, :])
    new_world_ref[...] = (lat.astype(F32) + message).astype(BF)
    world_sum = nn(put_dst[...], message.astype(BF)).astype(BF)

    for half in range(2):
        rows = slice(half * 512, half * 512 + 512)
        node = node_ref[rows, :]
        n_inputs = jnp.concatenate([node, sum_ref[rows, :], world_sum[rows, :]], axis=1)
        n_one = nn(n_inputs, first_ref[2]) + bias_ref[2, 0:1, :]
        n_sig_one, n_act_one, n_two, n_sig_two, n_act_two, n_centred, n_inv = layers(
            2, n_one, rest_ref, bias_ref
        )
        n_normed = n_centred * n_inv
        new_nodes_ref[rows, :] = (
            node.astype(F32) + n_normed * gain_ref[2:3, :] + bias_ref[2, 3:4, :]
        ).astype(BF)
        n_cot = node_cot_ref[rows, :].astype(F32)
        e_one, e_two, e_three, sums = layers_back(
            2, n_cot, n_one, n_sig_one, n_two, n_sig_two, n_normed, n_inv, rest_ref, gain_ref
        )
        g_first = tn(n_inputs, e_one)
        g_two = tn(n_act_one, e_two)
        g_three = tn(n_act_two, e_three)
        if half == 0:
            node_grad_ref[: 3 * D, :] = g_first
            node_grad_ref[3 * D : 4 * D, :] = g_two
            node_grad_ref[4 * D :, :] = g_three
            small_ref[8:, :] = sums
        else:
            node_grad_ref[: 3 * D, :] += g_first
            node_grad_ref[3 * D : 4 * D, :] += g_two
            node_grad_ref[4 * D :, :] += g_three
            small_ref[8:, :] += sums
        local_ref[rows, :] = n_cot + nt(e_one, first_ref[2, :D, :])
        mesh_back_ref[rows, :] = nt(e_one, first_ref[2, D : 2 * D, :]).astype(BF)
        world_back[rows, :] = nt(e_one, first_ref[2, 2 * D :, :]).astype(BF)

    own_cot = cot_ref[...].astype(F32)
    cot = keep * (own_cot + nn(pick_dst[...], world_back[...]))
    d_one, d_two, d_three, sums = layers_back(
        1, cot, pre_one, sig_one, pre_two, sig_two, normed, inv_std, rest_ref, gain_ref
    )
    small_ref[:8, :] = sums
    world_grad_ref[: 3 * D, :] = tn(inputs, d_one)
    world_grad_ref[3 * D : 4 * D, :] = tn(act_one, d_two)
    world_grad_ref[4 * D :, :] = tn(act_two, d_three)
    grad_world_ref[...] = (own_cot + nt(d_one, first_ref[1, :D, :])).astype(BF)
    to_source = nt(d_one, first_ref[1, D : 2 * D, :]).astype(BF)
    to_target = nt(d_one, first_ref[1, 2 * D :, :]).astype(BF)
    local_ref[...] += nn(put_dst[...], to_target)
    pick_columns(put_src, src_ref, 0, groups, 64)

    @pl.loop(0, 8)
    def _(b):
        rows = pl.ds(pl.multiple_of(b * 1024, 1024), 1024)
        back_ref[rows, :] = nn(put_src[rows, :], to_source).astype(BF)


def mesh_back_kernel(
    src_ref, dst_ref, node_ref, before_ref, after_ref, lat_ref, cot_ref, one_ref, two_ref,
    centred_ref, back_ref, part_ref, first_ref, rest_ref, gain_ref, grad_ref, left_ref, right_ref,
    local_ref, weight_ref, small_ref, pick_dst, put_src, put_dst, by_src, by_dst
):
    step = pl.program_id(0)
    groups = ROWS // 128
    first = step * groups
    pick_rows(pick_dst, dst_ref, first, groups, 8)
    pick_columns(put_src, src_ref, first, groups, 12)
    pick_columns(put_dst, dst_ref, first, groups, 8)
    lat = lat_ref[...]
    own_cot = cot_ref[...].astype(F32)
    cot = own_cot + nn(pick_dst[...], back_ref[...])
    pre_one = one_ref[...]
    pre_two = two_ref[...]
    centred = centred_ref[...]
    sig_one = sigma(pre_one)
    sig_two = sigma(pre_two)
    inv_std = lax.rsqrt(lane_mean(centred * centred) + EPS)
    normed = centred * inv_std
    d_one, d_two, d_three, sums = layers_back(
        0, cot, pre_one, sig_one, pre_two, sig_two, normed, inv_std, rest_ref, gain_ref
    )
    grad_ref[...] = (own_cot + nt(d_one, first_ref[0, :D, :])).astype(BF)
    g_lat = tn(lat, d_one)
    g_two = tn((pre_one * sig_one).astype(BF), d_two)
    g_three = tn((pre_two * sig_two).astype(BF), d_three)
    s_src = nn(put_src[...], d_one)
    s_dst = nn(put_dst[...], d_one)

    @pl.when(step == 0)
    def _():
        weight_ref[:D, :] = g_lat
        weight_ref[3 * D : 4 * D, :] = g_two
        weight_ref[4 * D :, :] = g_three
        small_ref[...] = sums
        by_src[...] = s_src
        by_dst[...] = s_dst

    @pl.when(step > 0)
    def _():
        weight_ref[:D, :] += g_lat
        weight_ref[3 * D : 4 * D, :] += g_two
        weight_ref[4 * D :, :] += g_three
        small_ref[...] += sums
        by_src[...] += s_src
        by_dst[...] += s_dst

    @pl.when(step == pl.num_programs(0) - 1)
    def _():
        src_sum = by_src[...].astype(BF)
        dst_sum = by_dst[...].astype(BF)
        weight_src = first_ref[0, D : 2 * D, :]
        left_ref[...] = nt(src_sum[:HALO], weight_src).astype(BF)
        right_ref[...] = nt(src_sum[HALO + 1024 :], weight_src).astype(BF)
        inner = src_sum[HALO : HALO + 1024]
        local_ref[...] = part_ref[...] + nt(inner, weight_src) + nt(dst_sum, first_ref[0, 2 * D :, :])
        weight_ref[D : 2 * D, :] = (
            tn(before_ref[...], src_sum[:HALO])
            + tn(node_ref[...], inner)
            + tn(after_ref[...], src_sum[HALO + 1024 :])
        )
        weight_ref[2 * D : 3 * D, :] = tn(node_ref[...], dst_sum)


def final_kernel(blocks_ref, part_ref, returned_ref, left_ref, right_ref, out_ref, total):
    total[...] = part_ref[...]
    total[:HALO, :] += left_ref[...].astype(F32)
    total[1024 - HALO :, :] += right_ref[...].astype(F32)

    @pl.loop(0, 512, unroll=4)
    def _(i):
        rows = pl.ds(pl.multiple_of(blocks_ref[i] * BLK, BLK), BLK)
        total[rows, :] += returned_ref[pl.ds(pl.multiple_of(i * BLK, BLK), BLK), :].astype(F32)

    out_ref[...] = total[...].astype(BF)


def reduce_kernel(
    n_dom, n_dp, mesh_ref, world_ref, node_ref, mesh_small_ref, other_small_ref, out_ref, sent,
    got, pair, sent_1, got_1, sent_2, got_2, sent_3, got_3
):
    dom = lax.axis_index("dom")
    dp = lax.axis_index("dp")
    rows = GRADS // n_dom
    barrier = pltpu.get_barrier_semaphore()

    @pl.loop(1, n_dom)
    def _(s):
        pl.semaphore_signal(
            barrier, inc=1, device_id=(lax.rem(dom + s, n_dom), dp), device_id_type=MESH
        )

    @pl.loop(1, n_dp)
    def _(s):
        pl.semaphore_signal(
            barrier, inc=1, device_id=(dom, lax.rem(dp + s, n_dp)), device_id_type=MESH
        )

    sent[:640, :] = mesh_ref[...].astype(BF)
    sent[640:1280, :] = world_ref[...].astype(BF)
    sent[1280:1920, :] = node_ref[...].astype(BF)
    sent[1920:, :] = jnp.concatenate(
        [mesh_small_ref[...], other_small_ref[...], jnp.zeros((104, D), F32)], axis=0
    ).astype(BF)
    pl.semaphore_wait(barrier, n_dom - 1 + n_dp - 1)

    def span(which):
        return pl.ds(pl.multiple_of(which * rows, rows), rows)

    def scatter(s):
        to = lax.rem(dom + s, n_dom)
        return pltpu.make_async_remote_copy(
            src_ref=sent.at[span(to)], dst_ref=got.at[span(dom)], send_sem=sent_1.at[s],
            recv_sem=got_1.at[s], device_id=(to, dp), device_id_type=MESH,
        )

    def swap(s):
        return pltpu.make_async_remote_copy(
            src_ref=pair.at[span(dp)], dst_ref=pair.at[span(dp)], send_sem=sent_2.at[s],
            recv_sem=got_2.at[s], device_id=(dom, lax.rem(dp + s, n_dp)), device_id_type=MESH,
        )

    def spread(s):
        return pltpu.make_async_remote_copy(
            src_ref=out_ref.at[span(dom)], dst_ref=out_ref.at[span(dom)], send_sem=sent_3.at[s],
            recv_sem=got_3.at[s], device_id=(lax.rem(dom + s, n_dom), dp), device_id_type=MESH,
        )

    @pl.loop(1, n_dom)
    def _(s):
        scatter(s).start()

    def collect(s, total):
        scatter(s).wait_recv()
        return total + got[span(lax.rem(dom - s + n_dom, n_dom)), :].astype(F32)

    total = lax.fori_loop(1, n_dom, collect, sent[span(dom), :].astype(F32))
    pair[span(dp), :] = total.astype(BF)
    for s in range(1, n_dp):
        swap(s).start()
    for s in range(1, n_dp):
        swap(s).wait_recv()
    total = pair[:rows, :].astype(F32)
    for i in range(1, n_dp):
        total = total + pair[i * rows : (i + 1) * rows, :].astype(F32)
    out_ref[span(dom), :] = (total * (1.0 / (n_dom * n_dp))).astype(BF)

    @pl.loop(1, n_dom)
    def _(s):
        spread(s).start()

    @pl.loop(1, n_dom)
    def _(s):
        scatter(s).wait_send()
        spread(s).wait()

    for s in range(1, n_dp):
        swap(s).wait_send()


def whole(shape):
    return pl.BlockSpec(shape, lambda i: (0,) * len(shape))


def blocked(rows):
    return pl.BlockSpec((rows, D), lambda i: (i, 0))


VMEM = pl.BlockSpec(memory_space=pltpu.VMEM)
SMEM = pl.BlockSpec(memory_space=pltpu.SMEM)
PARAMS = dict(vmem_limit_bytes=58 * 1024 * 1024)


def shape(rows, dtype):
    return jax.ShapeDtypeStruct((rows, D), dtype)


def per_device(
    node_latents,
    mesh_latents,
    world_latents,
    mesh_src,
    mesh_dst,
    world_src,
    world_dst,
    send_blocks,
    world_count,
    node_cot,
    mesh_cot,
    world_cot,
    first_weights,
    rest_weights,
    biases,
    gains,
):
    n_dom = lax.axis_size("dom")
    n_dp = lax.axis_size("dp")
    n_mesh = mesh_latents.shape[0]
    steps = n_mesh // ROWS
    up = [(i, i + 1) for i in range(n_dom - 1)]
    down = [(j, i) for i, j in up]
    blocks = send_blocks.reshape(-1)
    src = mesh_src.reshape(-1, 128)
    dst = mesh_dst.reshape(-1, 128)
    w_src = world_src.reshape(-1, 128)
    w_dst = world_dst.reshape(-1, 128)

    before = lax.ppermute(node_latents[1024 - HALO :], "dom", up)
    after = lax.ppermute(node_latents[:HALO], "dom", down)
    sending = pl.pallas_call(
        prep_kernel,
        out_shape=shape(8192, BF),
        in_specs=[SMEM, VMEM],
        out_specs=VMEM,
        cost_estimate=pl.CostEstimate(flops=0, bytes_accessed=4 << 20, transcendentals=0),
        name="prep",
    )(blocks, node_latents)
    incoming = lax.all_to_all(sending, "dom", split_axis=0, concat_axis=0, tiled=True)

    weight_specs = [
        whole((3, 3 * D, D)), whole((3, 2, D, D)), whole((3, 4, D)), whole((3, D)),
    ]
    index = whole((n_mesh // 128, 128))
    new_mesh, mesh_sum, pre_one, pre_two, centred = pl.pallas_call(
        mesh_kernel,
        grid=(steps,),
        out_shape=[shape(n_mesh, BF), shape(1024, BF)] + [shape(n_mesh, F32)] * 3,
        in_specs=[index, index, whole((1024, D)), whole((HALO, D)), whole((HALO, D)), blocked(ROWS)]
        + weight_specs,
        out_specs=[blocked(ROWS), whole((1024, D))] + [blocked(ROWS)] * 3,
        scratch_shapes=[
            pltpu.VMEM((ROWS, 1536), BF),
            pltpu.VMEM((ROWS, 1024), BF),
            pltpu.VMEM((1024, ROWS), BF),
            pltpu.VMEM((1024, D), F32),
        ],
        compiler_params=pltpu.CompilerParams(**PARAMS),
        cost_estimate=pl.CostEstimate(flops=8 << 30, bytes_accessed=8 << 20, transcendentals=1 << 20),
        name="mesh_forward",
    )(src, dst, node_latents, before, after, mesh_latents, first_weights, rest_weights, biases, gains)

    (
        new_nodes, new_world, grad_world, back, mesh_back, part, world_grad, node_grad, small
    ) = pl.pallas_call(
        middle_kernel,
        out_shape=[
            shape(1024, BF), shape(512, BF), shape(512, BF), shape(8192, BF), shape(1024, BF),
            shape(1024, F32), shape(640, F32), shape(640, F32), shape(16, F32),
        ],
        in_specs=[SMEM] + [VMEM] * 12,
        out_specs=[VMEM] * 9,
        scratch_shapes=[
            pltpu.VMEM((512, 8192), BF),
            pltpu.VMEM((512, 1024), BF),
            pltpu.VMEM((8192, 512), BF),
            pltpu.VMEM((1024, 512), BF),
            pltpu.VMEM((1024, D), BF),
        ],
        compiler_params=pltpu.CompilerParams(**PARAMS),
        cost_estimate=pl.CostEstimate(flops=4 << 30, bytes_accessed=8 << 20, transcendentals=1 << 20),
        name="world_and_nodes",
    )(
        world_count, w_src, w_dst, node_latents, incoming, world_latents, world_cot, mesh_sum,
        node_cot, first_weights, rest_weights, biases, gains,
    )
    returned = lax.all_to_all(back, "dom", split_axis=0, concat_axis=0, tiled=True)

    grad_mesh, left, right, local, mesh_grad, mesh_small = pl.pallas_call(
        mesh_back_kernel,
        grid=(steps,),
        out_shape=[
            shape(n_mesh, BF), shape(HALO, BF), shape(HALO, BF), shape(1024, F32),
            shape(640, F32), shape(8, F32),
        ],
        in_specs=[index, index, whole((1024, D)), whole((HALO, D)), whole((HALO, D))]
        + [blocked(ROWS)] * 5
        + [whole((1024, D)), whole((1024, D)), weight_specs[0], weight_specs[1], weight_specs[3]],
        out_specs=[
            blocked(ROWS), whole((HALO, D)), whole((HALO, D)), whole((1024, D)), whole((640, D)),
            whole((8, D)),
        ],
        scratch_shapes=[
            pltpu.VMEM((ROWS, 1024), BF),
            pltpu.VMEM((1536, ROWS), BF),
            pltpu.VMEM((1024, ROWS), BF),
            pltpu.VMEM((1536, D), F32),
            pltpu.VMEM((1024, D), F32),
        ],
        compiler_params=pltpu.CompilerParams(**PARAMS),
        cost_estimate=pl.CostEstimate(flops=8 << 30, bytes_accessed=8 << 20, transcendentals=1 << 20),
        name="mesh_backward",
    )(
        src, dst, node_latents, before, after, mesh_latents, mesh_cot, pre_one, pre_two, centred,
        mesh_back, part, first_weights, rest_weights, gains,
    )
    from_right = lax.ppermute(left, "dom", down)
    from_left = lax.ppermute(right, "dom", up)

    def dma(count):
        return pltpu.SemaphoreType.DMA((count,))

    packed = pl.pallas_call(
        functools.partial(reduce_kernel, n_dom, n_dp),
        out_shape=shape(GRADS, BF),
        in_specs=[VMEM] * 5,
        out_specs=VMEM,
        scratch_shapes=[
            pltpu.VMEM((GRADS, D), BF),
            pltpu.VMEM((GRADS, D), BF),
            pltpu.VMEM((n_dp * GRADS // n_dom, D), BF),
            dma(n_dom), dma(n_dom), dma(n_dp), dma(n_dp), dma(n_dom), dma(n_dom),
        ],
        compiler_params=pltpu.CompilerParams(collective_id=0, has_side_effects=True),
        name="reduce_grads",
    )(mesh_grad, world_grad, node_grad, mesh_small, small)

    grad_nodes = pl.pallas_call(
        final_kernel,
        out_shape=shape(1024, BF),
        in_specs=[SMEM] + [VMEM] * 4,
        out_specs=VMEM,
        scratch_shapes=[pltpu.VMEM((1024, D), F32)],
        name="gather_gradients",
    )(blocks, local, returned, from_left, from_right)

    big = packed[:1920].astype(F32).reshape(3, 640, D)
    tiny = packed[1920:1944].astype(F32).reshape(3, 8, D)
    return (
        new_nodes,
        new_mesh,
        new_world,
        grad_nodes,
        grad_mesh,
        grad_world,
        big[:, : 3 * D],
        big[:, 3 * D :].reshape(3, 2, D, D),
        tiny[:, :4],
        tiny[:, 4],
    )


def solution(mesh):
    part = P(("dom", "dp"))
    rows = P(("dom", "dp"), None)
    return jax.shard_map(
        per_device,
        mesh=mesh,
        in_specs=(
            rows, rows, rows, part, part, part, part, P(("dom", "dp"), None, None), part, rows,
            rows, rows, P(), P(), P(), P(),
        ),
        out_specs=(rows, rows, rows, rows, rows, rows, P(), P(), P(), P()),
        check_vma=False,
    )
```

time: 455 us -> 157 us (0.35); the launches traced: 447 us -> 157 us
  other arithmetic: 136 us -> 0.7 us
  Pallas kernels: 0 us -> 98.4 us
  local copies, waits for them, and re-layouts: 101 us -> 8.59 us
  blocking collectives: 67.1 us -> 0 us
  waiting for transfers between devices: 60.6 us -> 19.6 us
  matrix products: 37.3 us -> 0 us
  between operations: 16.5 us -> 1.43 us
    scatter-add x7 -> x0, other arithmetic: 107 us -> none  [the longest x1 44.8 us: per_device(): jax.ops.segment_sum(returned, send_index, num_segments=node_count)]
    pallas_call x0 -> x6, Pallas kernels: none -> 98.4 us  [the longest x1 30.8 us: per_device(): pl.pallas_call(functools.partial(reduce_kernel, n_dom, n_dp), out_shape=s...]
    gather x9 -> x0, local copies, waits for them, and re-layouts: 72.8 us -> none  [the longest x1 29.5 us: per_device(): node_latents[send_index]]
    psum x1 -> x0, blocking collectives: 67.1 us -> none  [per_device(): lax.psum((jnp.stack([mesh_grads[0], weight_grads[0], node_grads[0]]), jnp...]
    psum x1 -> x0, waiting for transfers between devices: 50 us -> none  [per_device(): lax.psum((jnp.stack([mesh_grads[0], weight_grads[0], node_grads[0]]), jnp...]
    dot_general x27 -> x0, matrix products: 37.3 us -> none  [the longest x9 16.3 us: matmul_nt(): lax.dot_general(left, right, (((1,), (1,)), ((), ())), preferred_element_...]
    unnamed x194 -> x16, local copies, waits for them, and re-layouts: 18.2 us -> 4.68 us
    convert_element_type x9 -> x0, other arithmetic: 9.15 us -> none  [the longest x1 3.71 us: per_device(): to_source.astype(jnp.bfloat16)]
  transfers between devices with their start and end apart: 7 -> 6, of which waited for: 3 -> 1; matrix products, arithmetic and copies ran while one was open for 29% -> 3% of each run, Pallas kernels for 0% -> 42%
where the time goes in v1:
time: 157 us
  Pallas kernels  98.4 us (63%)
  starting transfers between devices  28 us (18%)
  waiting for transfers between devices  19.6 us (12%)
  local copies, waits for them, and re-layouts  8.59 us (5%)
    pallas_call x1, Pallas kernels, per_device(): pl.pallas_call(functools.partial(reduce_kernel, n_dom, n_dp), out_shape=s...  30.8 us
    pallas_call x1, Pallas kernels, per_device(): pl.pallas_call(middle_kernel, out_shape=[shape(1024, BF), shape(512, BF),...  24.4 us
    ppermute x1, waiting for transfers between devices, per_device(): after = lax.ppermute(node_latents[:HALO], 'dom', down)  19.6 us
    pallas_call x1, Pallas kernels, per_device(): pl.pallas_call(mesh_back_kernel, grid=(steps,), out_shape=[shape(n_mesh,...  17.4 us
    pallas_call x1, Pallas kernels, per_device(): pl.pallas_call(mesh_kernel, grid=(steps,), out_shape=[shape(n_mesh, BF),...  17.3 us
    all_to_all x1, starting transfers between devices, per_device(): lax.all_to_all(sending, 'dom', split_axis=0, concat_axis=0, tiled=True)  9.56 us
    all_to_all x1, starting transfers between devices, per_device(): lax.all_to_all(back, 'dom', split_axis=0, concat_axis=0, tiled=True)  7.44 us
    unnamed x16, local copies, waits for them, and re-layouts  4.68 us
  transfers between devices with their start and end apart: 6, of which 1 were waited for; matrix products, arithmetic and copies ran while one was open for 3% of the time, Pallas kernels for 42%

profile of v1, /device:TPU:1, one launch (start us, length us, event | category | flops | bytes accessed | tf_op | source)
XLA Modules:
  0.0 156.8 jit_solution(1315487751529922786)
XLA Ops:
  0.6 0.8 copy.27
  1.4 0.6 reshape.56.blocks_ref
  2.0 4.0 %prep.1 = bf16[8192,128]{1,0:T(8,128)(2,1)} custom-call(s32[512]{0:T(512)} %reshape.56.blocks_ref, bf16[1024,128]{1,0:T(8,128)(2,1)} %node_ref.7), custom_call_target="tpu_custom_call" | custom-call | bytes 4194304 | tf_op jit(solution)/shard_map/prep/pallas_call | solution.py:463
  6.0 0.0 copy-start.2
  6.0 9.6 %all-to-all-start = ((bf16[32,256,128]{2,1,0:T(8,128)(2,1)}), bf16[32,256,128]{2,1,0:T(8,128)(2,1)S(1)}, u32[]{:S(2)}, u32[]{:S(2)}) async-start(bf16[32,256,128]{2,1,0:T(8,128)(2,1)} %bitcast.18), calls=%async_computation | async-start | bytes 4194304 | tf_op jit(solution)/shard_map/all_to_all | solution.py:471
  15.6 0.0 copy-done.2
  15.6 2.1 %collective-permute-start.1 = (bf16[256,128]{1,0:T(8,128)(2,1)S(1)}, bf16[256,128]{1,0:T(8,128)(2,1)S(1)}, u32[]{:S(2)}, u32[]{:S(2)}) collective-permute-start(bf16[256,128]{1,0:T(8,128)(2,1)S(1)} %get-tuple-element.50), channel_id=1, source_target_pairs={{4,0},{8,4},{12,8},{16,12},{20,16},{24,20},{28,24},{32,28},{36,32}... | collective-permute-start | bytes 196616 | tf_op jit(solution)/shard_map/ppermute | solution.py:462
  17.8 3.4 %collective-permute-start = (bf16[256,128]{1,0:T(8,128)(2,1)S(1)}, bf16[256,128]{1,0:T(8,128)(2,1)S(1)}, u32[]{:S(2)}, u32[]{:S(2)}) collective-permute-start(bf16[256,128]{1,0:T(8,128)(2,1)S(1)} %get-tuple-element.51), channel_id=1, source_target_pairs={{0,4},{4,8},{8,12},{12,16},{16,20},{20,24},{24,28},{28,32},{32,36}... | collective-permute-start | bytes 196616 | tf_op jit(solution)/shard_map/ppermute | solution.py:461
  21.8 19.6 %collective-permute-done.1.after_ref = bf16[256,128]{1,0:T(8,128)(2,1)S(1)} collective-permute-done((bf16[256,128]{1,0:T(8,128)(2,1)S(1)}, bf16[256,128]{1,0:T(8,128)(2,1)S(1)}, u32[]{:S(2)}, u32[]{:S(2)}) %collective-permute-start.1) | collective-permute-done | bytes 65568 | tf_op jit(solution)/shard_map/ppermute | solution.py:462
  41.4 0.0 copy-start.5
  41.4 0.0 collective-permute-done.before_ref
  41.4 0.0 copy-start.6
  41.4 0.6 copy-done.5
  42.1 0.0 copy-done.6
  42.1 17.3 %mesh_forward.1 = (bf16[3072,128]{1,0:T(8,128)(2,1)}, bf16[1024,128]{1,0:T(8,128)(2,1)}, f32[3072,128]{1,0:T(8,128)}, f32[3072,128]{1,0:T(8,128)}, f32[3072,128]{1,0:T(8,128)}) custom-call(s32[24,128]{1,0:T(8,128)} %bitcast.25, s32[24,128]{1,0:T(8,128)} %bitcast.27, bf16[1024,128]{1,0:T(8,128)(2,1)} %node_ref.7, bf16[256,128]{1,0:T(8,128)(2,1)} %copy-done.6, ...), custom_call_target="tpu_custom_call" | custom-call | flops 8589934592 | bytes 8388608 | tf_op jit(solution)/shard_map/mesh_forward/pallas_call | solution.py:477
  59.4 0.0 all-to-all-done
  59.4 0.0 copy-start.1
  59.4 1.3 copy-done.1
  60.7 24.4 %world_and_nodes.1 = (bf16[1024,128]{1,0:T(8,128)(2,1)}, bf16[512,128]{1,0:T(8,128)(2,1)}, bf16[512,128]{1,0:T(8,128)(2,1)}, bf16[8192,128]{1,0:T(8,128)(2,1)}, ...) custom-call(s32[1]{0:T(128)S(6)} %copy.32.count_ref, ...), custom_call_target="tpu_custom_call" | custom-call | flops 4294967296 | bytes 8388608 | tf_op jit(solution)/shard_map/world_and_nodes/pallas_call | solution.py:497
  85.2 7.4 %all-to-all-start.1 = ((bf16[32,256,128]{2,1,0:T(8,128)(2,1)}), bf16[32,256,128]{2,1,0:T(8,128)(2,1)S(1)}, u32[]{:S(2)}, u32[]{:S(2)}) async-start(bf16[32,256,128]{2,1,0:T(8,128)(2,1)} %bitcast.21), calls=%async_computation.1 | async-start | bytes 4194304 | tf_op jit(solution)/shard_map/all_to_all | solution.py:519
  92.6 17.4 %mesh_backward.1 = (bf16[3072,128]{1,0:T(8,128)(2,1)}, bf16[256,128]{1,0:T(8,128)(2,1)}, bf16[256,128]{1,0:T(8,128)(2,1)}, f32[1024,128]{1,0:T(8,128)}, f32[640,128]{1,0:T(8,128)}, /*index=5*/f32[8,128]{1,0:T(8,128)}) custom-call(s32[24,128]{1,0:T(8,128)} %bitcast.26, s32[24,128]{1,0:T(8,128)} %bitcast.28, bf16[1024,128]{1,0:T(8,128)(2,1)} %node_ref.7, ...), custom_call_target="tpu_custom_call" | custom-call | flops 8589934592 | bytes 8388608 | tf_op jit(solution)/shard_map/mesh_backward/pallas_call | solution.py:521
  110.0 3.5 %collective-permute-start.2 = (bf16[256,128]{1,0:T(8,128)(2,1)}, bf16[256,128]{1,0:T(8,128)(2,1)S(1)}, u32[]{:S(2)}, u32[]{:S(2)}) collective-permute-start(bf16[256,128]{1,0:T(8,128)(2,1)} %get-tuple-element.41), channel_id=1, source_target_pairs={{0,4},{4,8},{8,12},{12,16},{16,20},{20,24},{24,28},{28,32},{32,36}... | collective-permute-start | bytes 196616 | tf_op jit(solution)/shard_map/ppermute | solution.py:550
  113.6 1.9 %collective-permute-start.3 = (bf16[256,128]{1,0:T(8,128)(2,1)}, bf16[256,128]{1,0:T(8,128)(2,1)S(1)}, u32[]{:S(2)}, u32[]{:S(2)}) collective-permute-start(bf16[256,128]{1,0:T(8,128)(2,1)} %get-tuple-element.42), channel_id=1, source_target_pairs={{4,0},{8,4},{12,8},{16,12},{20,16},{24,20},{28,24},{32,28},{36,32}... | collective-permute-start | bytes 196616 | tf_op jit(solution)/shard_map/ppermute | solution.py:549
  115.5 30.8 %reduce_grads.1 = bf16[2048,128]{1,0:T(8,128)(2,1)} custom-call(f32[640,128]{1,0:T(8,128)} %get-tuple-element.45.mesh_ref, f32[640,128]{1,0:T(8,128)} %get-tuple-element.46.world_ref, f32[640,128]{1,0:T(8,128)} %get-tuple-element.47.node_ref, f32[8,128]{1,0:T(8,128)} %get-tuple-element.48.mesh_small_ref, f32[16,128]{1,0:T(8,128)} %get-tuple-element.49.other_small_ref), custom_call_target="tpu_custom_call" | custom-call | tf_op jit(solution)/shard_map/reduce_grads/pallas_call | solution.py:555
  146.3 0.7 bitcast_convert_fusion
  147.0 1.1 slice.26
  148.1 0.6 slice.34
  148.7 0.8 slice.33
  149.4 0.9 slice.32
  150.3 0.6 copy.31
  150.9 0.0 collective-permute-done.2.left_ref
  150.9 0.0 copy-start.3
  150.9 0.0 collective-permute-done.3.right_ref
  150.9 0.0 copy-start.4
  150.9 0.0 all-to-all-done.1
  150.9 0.0 copy-start
  150.9 0.6 copy-done.3
  151.5 0.0 copy-done.4
  151.5 0.7 copy-done
  152.2 4.5 %gather_gradients.1 = bf16[1024,128]{1,0:T(8,128)(2,1)} custom-call(s32[512]{0:T(512)} %reshape.56.blocks_ref, f32[1024,128]{1,0:T(8,128)} %get-tuple-element.39.part_ref, bf16[8192,128]{1,0:T(8,128)(2,1)} %bitcast.17, bf16[256,128]{1,0:T(8,128)(2,1)} %copy-done.3, bf16[256,128]{1,0:T(8,128)(2,1)} %copy-done.4), custom_call_target="tpu_custom_call" | custom-call | tf_op jit(solution)/shard_map/gather_gradients/pallas_call | solution.py:570
  (2 shorter events, 0.0 us)
Async XLA Ops:
  6.0 9.6 %copy-start.2 = (bf16[1024,128]{1,0:T(8,128)(2,1)S(1)}, bf16[1024,128]{1,0:T(8,128)(2,1)}, u32[]{:S(2)}) copy-start(bf16[1024,128]{1,0:T(8,128)(2,1)} %node_ref.7) | copy-start | bytes 786436
  6.0 53.4 %all-to-all-start = ((bf16[32,256,128]{2,1,0:T(8,128)(2,1)}), bf16[32,256,128]{2,1,0:T(8,128)(2,1)S(1)}, u32[]{:S(2)}, u32[]{:S(2)}) async-start(bf16[32,256,128]{2,1,0:T(8,128)(2,1)} %bitcast.18), calls=%async_computation | async-start | bytes 4194304 | tf_op jit(solution)/shard_map/all_to_all | solution.py:471
  15.6 25.8 %collective-permute-start.1 = (bf16[256,128]{1,0:T(8,128)(2,1)S(1)}, bf16[256,128]{1,0:T(8,128)(2,1)S(1)}, u32[]{:S(2)}, u32[]{:S(2)}) collective-permute-start(bf16[256,128]{1,0:T(8,128)(2,1)S(1)} %get-tuple-element.50), channel_id=1, source_target_pairs={{4,0},{8,4},{12,8},{16,12},{20,16},{24,20},{28,24},{32,28},{36,32}... | collective-permute-start | bytes 196616 | tf_op jit(solution)/shard_map/ppermute | solution.py:462
  17.8 23.7 %collective-permute-start = (bf16[256,128]{1,0:T(8,128)(2,1)S(1)}, bf16[256,128]{1,0:T(8,128)(2,1)S(1)}, u32[]{:S(2)}, u32[]{:S(2)}) collective-permute-start(bf16[256,128]{1,0:T(8,128)(2,1)S(1)} %get-tuple-element.51), channel_id=1, source_target_pairs={{0,4},{4,8},{8,12},{12,16},{16,20},{20,24},{24,28},{28,32},{32,36}... | collective-permute-start | bytes 196616 | tf_op jit(solution)/shard_map/ppermute | solution.py:461
  41.4 0.6 copy-start.5
  41.4 0.7 copy-start.6
  59.4 1.3 copy-start.1
  85.2 65.7 %all-to-all-start.1 = ((bf16[32,256,128]{2,1,0:T(8,128)(2,1)}), bf16[32,256,128]{2,1,0:T(8,128)(2,1)S(1)}, u32[]{:S(2)}, u32[]{:S(2)}) async-start(bf16[32,256,128]{2,1,0:T(8,128)(2,1)} %bitcast.21), calls=%async_computation.1 | async-start | bytes 4194304 | tf_op jit(solution)/shard_map/all_to_all | solution.py:519
  110.0 40.8 %collective-permute-start.2 = (bf16[256,128]{1,0:T(8,128)(2,1)}, bf16[256,128]{1,0:T(8,128)(2,1)S(1)}, u32[]{:S(2)}, u32[]{:S(2)}) collective-permute-start(bf16[256,128]{1,0:T(8,128)(2,1)} %get-tuple-element.41), channel_id=1, source_target_pairs={{0,4},{4,8},{8,12},{12,16},{16,20},{20,24},{24,28},{28,32},{32,36}... | collective-permute-start | bytes 196616 | tf_op jit(solution)/shard_map/ppermute | solution.py:550
  113.6 37.3 %collective-permute-start.3 = (bf16[256,128]{1,0:T(8,128)(2,1)}, bf16[256,128]{1,0:T(8,128)(2,1)S(1)}, u32[]{:S(2)}, u32[]{:S(2)}) collective-permute-start(bf16[256,128]{1,0:T(8,128)(2,1)} %get-tuple-element.42), channel_id=1, source_target_pairs={{4,0},{8,4},{12,8},{16,12},{20,16},{24,20},{28,24},{32,28},{36,32}... | collective-permute-start | bytes 196616 | tf_op jit(solution)/shard_map/ppermute | solution.py:549
  150.9 0.6 copy-start.3
  150.9 0.6 copy-start.4
  150.9 1.3 copy-start

commit v2 on v0

--- a/solution.py
+++ b/solution.py
@@ -1,13 +1,245 @@
+import functools
+
 import jax
 import jax.numpy as jnp
 from jax import lax
+from jax.experimental import pallas as pl
+from jax.experimental.pallas import tpu as pltpu
 from jax.sharding import PartitionSpec as P
 
+D = 128
 HALO = 256
 BLK = 16
-
-
-norm_eps = 1e-05
+ROWS = 512
+GROUPS = ROWS // 128
+NODES = 1024
+CAP = 48
+LATE = 32
+EARLY = 16
+QUARTER = 320
+N_LATE = 672
+EPS = 1e-05
+BF = jnp.bfloat16
+F32 = jnp.float32
+MESH = pl.DeviceIdType.MESH
+
+
+def nn(left, right):
+    return jnp.dot(left, right, preferred_element_type=F32)
+
+
+def nt(left, right):
+    return lax.dot_general(left, right, (((1,), (1,)), ((), ())), preferred_element_type=F32)
+
+
+def tn(left, right):
+    return lax.dot_general(left, right, (((0,), (0,)), ((), ())), preferred_element_type=F32)
+
+
+def sigma(values):
+    return 0.5 + 0.5 * jnp.tanh(0.5 * values)
+
+
+def lane_mean(values):
+    return jnp.sum(values, axis=-1, keepdims=True) * (1.0 / D)
+
+
+def columns_of(index_ref, first):
+    return [
+        jnp.transpose(jnp.broadcast_to(index_ref[pl.ds(first + g, 1), :], (128, 128)))
+        for g in range(GROUPS)
+    ]
+
+
+def load_columns(columns_ref, first):
+    return [columns_ref[pl.ds(pl.multiple_of(first + g * 128, 128), 128), :] for g in range(GROUPS)]
+
+
+def fold(index, half):
+    return jnp.where(index >= half, index - half, index)
+
+
+def pick(columns, half):
+    lane = lax.broadcasted_iota(jnp.int32, (128, 128), 1).astype(jnp.int16)
+    one = jnp.ones((128, 128), BF)
+    zero = jnp.zeros((128, 128), BF)
+    out = []
+    for column in columns:
+        low = fold(column, half).astype(jnp.int16)
+        out.append(
+            jnp.concatenate(
+                [jnp.where(low == lane + jnp.int16(b * 128), one, zero) for b in range(half // 128)],
+                axis=1,
+            )
+        )
+    return jnp.concatenate(out, axis=0)
+
+
+def put(index_ref, first, half):
+    down = lax.broadcasted_iota(jnp.int32, (128, 128), 0).astype(jnp.int16)
+    one = jnp.ones((128, 128), BF)
+    zero = jnp.zeros((128, 128), BF)
+    out = []
+    for g in range(GROUPS):
+        row = fold(index_ref[pl.ds(first + g, 1), :], half)
+        low = jnp.broadcast_to(row, (128, 128)).astype(jnp.int16)
+        out.append(
+            jnp.concatenate(
+                [jnp.where(low == down + jnp.int16(b * 128), one, zero) for b in range(half // 128)],
+                axis=0,
+            )
+        )
+    return jnp.concatenate(out, axis=1)
+
+
+def gathered(picked, columns, half, table):
+    both = nn(picked, table)
+    return jnp.concatenate(
+        [
+            jnp.where(
+                column >= half,
+                both[g * 128 : (g + 1) * 128, D:],
+                both[g * 128 : (g + 1) * 128, :D],
+            )
+            for g, column in enumerate(columns)
+        ],
+        axis=0,
+    )
+
+
+def halved(values, columns, half):
+    out = []
+    for g, column in enumerate(columns):
+        rows = values[g * 128 : (g + 1) * 128, :]
+        high = column >= half
+        out.append(
+            jnp.concatenate([jnp.where(high, 0.0, rows), jnp.where(high, rows, 0.0)], axis=1)
+        )
+    return jnp.concatenate(out, axis=0).astype(BF)
+
+
+def layers(which, pre_one, rest_ref, bias_ref):
+    sig_one = sigma(pre_one)
+    act_one = (pre_one * sig_one).astype(BF)
+    pre_two = nn(act_one, rest_ref[which, 0]) + bias_ref[which, 1:2, :]
+    sig_two = sigma(pre_two)
+    act_two = (pre_two * sig_two).astype(BF)
+    pre_three = nn(act_two, rest_ref[which, 1]) + bias_ref[which, 2:3, :]
+    centred = pre_three - lane_mean(pre_three)
+    inv_std = lax.rsqrt(lane_mean(centred * centred) + EPS)
+    return sig_one, act_one, pre_two, sig_two, act_two, centred, inv_std
+
+
+def layers_back(which, cot, pre_one, sig_one, pre_two, sig_two, normed, inv_std, rest_ref, gain_ref):
+    scaled = cot * gain_ref[which : which + 1, :]
+    d_three = inv_std * (scaled - lane_mean(scaled) - normed * lane_mean(scaled * normed))
+    d_three_b = d_three.astype(BF)
+    d_two = nt(d_three_b, rest_ref[which, 1]) * (sig_two * (1.0 + pre_two * (1.0 - sig_two)))
+    d_two_b = d_two.astype(BF)
+    d_one = nt(d_two_b, rest_ref[which, 0]) * (sig_one * (1.0 + pre_one * (1.0 - sig_one)))
+    d_one_b = d_one.astype(BF)
+
+    def total(values):
+        return jnp.sum(values, axis=0, keepdims=True)
+
+    sums = jnp.concatenate(
+        [
+            total(d_one),
+            total(d_two),
+            total(d_three),
+            total(cot),
+            total(cot * normed),
+            jnp.zeros((3, D), F32),
+        ],
+        axis=0,
+    )
+    return d_one_b, d_two_b, d_three_b, sums
+
+
+def span(which, rows):
+    return pl.ds(pl.multiple_of(which * rows, rows), rows)
+
+
+def greet(n_dom, n_dp, dom, dp, barrier):
+    @pl.loop(1, n_dom)
+    def _(s):
+        pl.semaphore_signal(
+            barrier, inc=1, device_id=(lax.rem(dom + s, n_dom), dp), device_id_type=MESH
+        )
+
+    @pl.loop(1, n_dp)
+    def _(s):
+        pl.semaphore_signal(
+            barrier, inc=1, device_id=(dom, lax.rem(dp + s, n_dp)), device_id_type=MESH
+        )
+
+
+def requests(count_ref, src_ref, slot_ref, ask_ref):
+    lane = lax.broadcasted_iota(jnp.int32, (1, 128), 1)
+    domain = lax.broadcasted_iota(jnp.int32, (32, 128), 0)
+    live_rows = count_ref[0]
+    owned, valued = [], []
+    for g in range(4):
+        row = src_ref[g : g + 1, :]
+        live = lane + g * 128 < live_rows
+        peer = jnp.where(live, row >> 8, -1)
+        hit = jnp.where(jnp.broadcast_to(peer, (32, 128)) == domain, 1.0, 0.0)
+        owned.append(hit)
+        valued.append(hit * ((row & 255) + 1).astype(F32))
+    owned = jnp.concatenate(owned, axis=1)
+    valued = jnp.concatenate(valued, axis=1).astype(BF)
+    earlier = lax.broadcasted_iota(jnp.int32, (512, 512), 0) < lax.broadcasted_iota(
+        jnp.int32, (512, 512), 1
+    )
+    ahead = nn(owned.astype(BF), jnp.where(earlier, 1.0, 0.0).astype(BF))
+    rank = jnp.sum(owned * ahead, axis=0, keepdims=True)
+    most = jnp.max(jnp.sum(owned, axis=1, keepdims=True), axis=0, keepdims=True)
+    place = lax.broadcasted_iota(jnp.int32, (128, 128), 1)
+    placed = []
+    for g in range(4):
+        row = src_ref[g : g + 1, :]
+        order = rank[:, g * 128 : (g + 1) * 128].astype(jnp.int32)
+        fits = jnp.logical_and(lane + g * 128 < live_rows, order < CAP)
+        slot_ref[g : g + 1, :] = jnp.where(fits, (row >> 8) * CAP + order, -1)
+        column = jnp.transpose(jnp.broadcast_to(order, (128, 128)))
+        placed.append(jnp.where(column == place, 1.0, 0.0).astype(BF))
+    table = nn(valued, jnp.concatenate(placed, axis=0))
+    wide = lax.broadcasted_iota(jnp.int32, (32, 128), 1)
+    table = jnp.where(wide < CAP, table, 0.0)
+    table = jnp.where(wide == 127, jnp.broadcast_to(most, (32, 128)), table).astype(jnp.int32)
+    for p in range(32):
+        ask_ref[p] = jnp.broadcast_to(table[p : p + 1, :], (8, 128))
+
+
+def asked_rows(asked_ref, blocks_ref, need_ref):
+    table = jnp.concatenate([asked_ref[k, 0:1, :] for k in range(32)], axis=0)
+    most = jnp.max(table[:, 127:128], axis=0, keepdims=True)
+    wanted = table - 1
+    slot = wanted >> 4
+    inside = wanted & 15
+    eye = lax.broadcasted_iota(jnp.int32, (16, 128), 0) == lax.broadcasted_iota(
+        jnp.int32, (16, 128), 1
+    )
+    blocks = tn(
+        blocks_ref[...].astype(F32).astype(BF), jnp.where(eye, 1.0, 0.0).astype(BF)
+    ).astype(jnp.int32)
+    rows = jnp.full((32, 128), -1, jnp.int32)
+    for t in range(16):
+        rows = jnp.where(slot == t, blocks[:, t : t + 1] * BLK + inside, rows)
+    rolled = {}
+    lane = lax.broadcasted_iota(jnp.int32, (1, 128), 1)
+    for g in range(32 * CAP // 128):
+        line = jnp.full((1, 128), -1, jnp.int32)
+        for k in range(32):
+            start = k * CAP - g * 128
+            if -CAP < start < 128:
+                if start % 128 not in rolled:
+                    rolled[start % 128] = pltpu.roll(rows, start % 128, 1) if start % 128 else rows
+                piece = rolled[start % 128][k : k + 1, :]
+                inside_piece = jnp.logical_and(lane >= start, lane < start + CAP)
+                line = jnp.where(inside_piece, piece, line)
+        need_ref[g : g + 1, :] = line
+    return most
 
 
 def extended(value, sides, width):
@@ -57,7 +289,7 @@
     act_two = jax.nn.silu(pre_two).astype(jnp.bfloat16)
     pre_three = matmul(act_two, rest_w[1]) + bias_rows[2]
     centred = pre_three - jnp.mean(pre_three, axis=-1, keepdims=True)
-    inv_std = lax.rsqrt(jnp.mean(centred * centred, axis=-1, keepdims=True) + norm_eps)
+    inv_std = lax.rsqrt(jnp.mean(centred * centred, axis=-1, keepdims=True) + EPS)
     normed = centred * inv_std
     output = normed * gain_row + bias_rows[3]
     return (output, (pre_one, act_one, pre_two, act_two, normed, inv_std))
@@ -89,7 +321,7 @@
     return (grad_in, (grad_w1, jnp.stack([grad_w2, grad_w3]), bias_grads, grad_gain))
 
 
-def per_device(
+def full_exchange(
     node_latents,
     mesh_latents,
     world_latents,
@@ -185,16 +417,25 @@
         grad_local + to_target + jax.ops.segment_sum(returned, send_index, num_segments=node_count)
     )
     grad_nodes = grad_local.astype(jnp.bfloat16)
-    divisor = lax.axis_size("dom") * lax.axis_size("dp")
-    summed_all = lax.psum(
-        (
-            jnp.stack([mesh_grads[0], weight_grads[0], node_grads[0]]),
-            jnp.stack([mesh_grads[1], weight_grads[1], node_grads[1]]),
-            jnp.stack([mesh_grads[2], weight_grads[2], node_grads[2]]),
+    packed = jnp.concatenate(
+        [
+            jnp.stack([mesh_grads[0], weight_grads[0], node_grads[0]]).reshape(-1, latent_width),
+            jnp.stack([mesh_grads[1], weight_grads[1], node_grads[1]]).reshape(-1, latent_width),
+            jnp.stack([mesh_grads[2], weight_grads[2], node_grads[2]]).reshape(-1, latent_width),
             jnp.stack([mesh_grads[3], weight_grads[3], node_grads[3]]),
-        ),
-        ("dom", "dp"),
-    )
+        ]
+    )
+    devices = lax.axis_size("dom") * lax.axis_size("dp")
+    used = packed.shape[0]
+    packed = jnp.pad(packed, ((0, -used % (8 * devices)), (0, 0)))
+    everyone = ("dom", "dp")
+    pieces = lax.all_to_all(packed, everyone, split_axis=0, concat_axis=0, tiled=True)
+    piece = jnp.sum(pieces.reshape(devices, -1, latent_width), axis=0) / devices
+    total = lax.all_to_all(
+        jnp.tile(piece, (devices, 1)), everyone, split_axis=0, concat_axis=0, tiled=True
+    )
+    first_rows = 9 * latent_width
+    rest_rows = first_rows + 6 * latent_width
     return (
         new_nodes,
         new_mesh,
@@ -202,46 +443,654 @@
         grad_nodes,
         grad_mesh,
         own_grad,
-        summed_all[0] / divisor,
-        summed_all[1] / divisor,
-        summed_all[2] / divisor,
-        summed_all[3] / divisor,
-    )
+        total[:first_rows].reshape(3, 3 * latent_width, latent_width),
+        total[first_rows:rest_rows].reshape(3, 2, latent_width, latent_width),
+        total[rest_rows : rest_rows + 12].reshape(3, 4, latent_width),
+        total[rest_rows + 12 : used],
+    )
+
+
+def cloth_kernel(
+    n_dom, n_dp, count_ref, wsrc_ref, wdst_ref, blocks_ref, src_ref, dst_ref, node_ref,
+    node_cot_ref, wlat_ref, wcot_ref, first_ref, rest_ref, bias_ref, gain_ref, lat_hbm, cot_hbm,
+    new_nodes_ref, new_world_ref, grad_nodes_ref, grad_world_ref, early_out, late_out, most_ref,
+    new_mesh_hbm, grad_mesh_hbm, lat_ref, cot_ref, new_ref, grad_ref, source_ref, target_ref,
+    one_ref, two_ref, centred_ref, d_ref, col_src, col_dst, col_need, pick_dst, put_dst, node2,
+    ext2, back2, world_back2, got_ref, got2, before_ref, after_ref, slot_ref, need_ref, ask_ref,
+    asked_ref, reply_ref, high_ref, acc_dst, acc_src, part2, weight_ref, sums_ref, sent_ref,
+    returned_ref, left_ref, right_ref, from_left_ref, from_right_ref, early, early_got, early_mid,
+    early_mid_got, tiny_ref, late, late_got, late_pair, in_s, out_s, ask_s, ask_r, reply_s, reply_r, halo_s, halo_r, high_s,
+    high_r, back_s, back_r, rim_s, rim_r, a_s, a_r, b_s, b_r, c_s, c_r, d_s,
+    d_r, e_s, e_r, f_s, f_r, g_s, g_r
+):
+    dom = lax.axis_index("dom")
+    dp = lax.axis_index("dp")
+    steps = lat_ref.shape[0] // ROWS
+    half = NODES // 2
+    wide = 768
+    slots = CAP * n_dom // 2
+    scale = 1.0 / (n_dom * n_dp)
+    barrier = pltpu.get_barrier_semaphore()
+    greet(n_dom, n_dp, dom, dp, barrier)
+    lat_in = pltpu.make_async_copy(lat_hbm, lat_ref, in_s.at[0])
+    cot_in = pltpu.make_async_copy(cot_hbm, cot_ref, in_s.at[1])
+    lat_in.start()
+    cot_in.start()
+    requests(count_ref, wsrc_ref, slot_ref, ask_ref)
+    pl.semaphore_wait(barrier, n_dom - 1 + n_dp - 1)
+
+    def new_out(c):
+        rows = span(c, ROWS)
+        return pltpu.make_async_copy(new_ref.at[rows], new_mesh_hbm.at[rows], out_s.at[0, c])
+
+    def grad_out(c):
+        rows = span(c, ROWS)
+        return pltpu.make_async_copy(grad_ref.at[rows], grad_mesh_hbm.at[rows], out_s.at[1, c])
+
+    def to_domain(from_ref, to_ref, sems, semr, s):
+        to = lax.rem(dom + s, n_dom)
+        return pltpu.make_async_remote_copy(
+            src_ref=from_ref(to), dst_ref=to_ref(dom), send_sem=sems.at[s], recv_sem=semr.at[s],
+            device_id=(to, dp), device_id_type=MESH,
+        )
+
+    def ask(s):
+        return to_domain(lambda to: ask_ref.at[to], lambda me: asked_ref.at[me], ask_s, ask_r, s)
+
+    def reply(s):
+        return to_domain(
+            lambda to: reply_ref.at[span(to, CAP)], lambda me: got_ref.at[span(me, CAP)],
+            reply_s, reply_r, s,
+        )
+
+    def give_back(s):
+        return to_domain(
+            lambda to: sent_ref.at[span(to, CAP)], lambda me: returned_ref.at[span(me, CAP)],
+            back_s, back_r, s,
+        )
+
+    def scatter(rows, mine, got, sems, semr, s):
+        return to_domain(
+            lambda to: mine.at[span(lax.rem(to, mine.shape[0] // rows), rows)],
+            lambda me: got.at[span(me, rows)], sems, semr, s,
+        )
+
+    def spread(rows, out, sems, semr, s):
+        at = span(lax.rem(dom, out.shape[0] // rows), rows)
+        return to_domain(lambda to: out.at[at], lambda me: out.at[at], sems, semr, s)
+
+    def swap(pair, sems, semr, s):
+        return pltpu.make_async_remote_copy(
+            src_ref=pair.at[dp], dst_ref=pair.at[dp], send_sem=sems.at[s], recv_sem=semr.at[s],
+            device_id=(dom, lax.rem(dp + s, n_dp)), device_id_type=MESH,
+        )
+
+    def neighbour(from_ref, to_ref, sems, semr, at, step):
+        return pltpu.make_async_remote_copy(
+            src_ref=from_ref, dst_ref=to_ref, send_sem=sems.at[at], recv_sem=semr.at[at],
+            device_id=(lax.rem(dom + step, n_dom), dp), device_id_type=MESH,
+        )
+
+    def collected(rows, mine, got, sems, semr):
+        def add(s, total):
+            scatter(rows, mine, got, sems, semr, s).wait_recv()
+            return total + got[span(lax.rem(dom - s + n_dom, n_dom), rows), :].astype(F32)
+
+        return lax.fori_loop(1, n_dom, add, mine[span(dom, rows), :].astype(F32))
+
+    def quarter(s):
+        to = lax.rem(dp + s, n_dp)
+        return pltpu.make_async_remote_copy(
+            src_ref=early.at[span(to, QUARTER)], dst_ref=early_got.at[span(dp, QUARTER)],
+            send_sem=a_s.at[s], recv_sem=a_r.at[s], device_id=(dom, to), device_id_type=MESH,
+        )
+
+    def middle(s):
+        return scatter(EARLY, early_mid, early_mid_got, b_s, b_r, s)
+
+    def mine():
+        return pl.ds(pl.multiple_of(dp * QUARTER + lax.rem(dom, QUARTER // EARLY) * EARLY, EARLY), EARLY)
+
+    def ready(s):
+        return to_domain(
+            lambda to: early_out.at[mine()], lambda me: early_out.at[mine()], c_s, c_r, s
+        )
+
+    def quarters(s):
+        rows = span(dp, QUARTER)
+        return pltpu.make_async_remote_copy(
+            src_ref=early_out.at[rows], dst_ref=early_out.at[rows], send_sem=g_s.at[s],
+            recv_sem=g_r.at[s], device_id=(dom, lax.rem(dp + s, n_dp)), device_id_type=MESH,
+        )
+
+    def paired(pair, sems, semr):
+        for s in range(1, n_dp):
+            swap(pair, sems, semr, s).wait_recv()
+        total = pair[0]
+        for i in range(1, n_dp):
+            total = total + pair[i]
+        return (total * scale).astype(BF)
+
+    halo_up = neighbour(
+        node_ref.at[pl.ds(NODES - HALO, HALO)], before_ref, halo_s, halo_r, 0, 1
+    )
+    halo_down = neighbour(node_ref.at[pl.ds(0, HALO)], after_ref, halo_s, halo_r, 1, n_dom - 1)
+
+
+    @pl.loop(1, n_dom)
+    def _(s):
+        ask(s).start()
+
+    halo_up.start()
+    halo_down.start()
+    asked_ref[dom] = ask_ref[dom]
+    node2[:, :D] = node_ref[:half, :]
+    node2[:, D:] = node_ref[half:, :]
+    ext2[HALO:, :D] = node_ref[:half, :]
+    ext2[:half, D:] = node_ref[half:, :]
+    acc_dst[...] = jnp.zeros(acc_dst.shape, F32)
+
+    @pl.loop(0, steps)
+    def _(c):
+        columns = columns_of(dst_ref, c * GROUPS)
+        rows = span(c, ROWS)
+        col_dst[rows, :] = jnp.concatenate(columns, axis=0)
+        picked = pick(columns, half)
+        pick_dst[rows, :] = picked
+        target_ref[rows, :] = gathered(picked, columns, half, node2[...]).astype(BF)
+
+    @pl.loop(1, n_dom)
+    def _(s):
+        ask(s).wait_recv()
+
+    high_ref[dp] = jnp.broadcast_to(asked_rows(asked_ref, blocks_ref, need_ref), (8, 128))
+    for s in range(1, n_dp):
+        swap(high_ref, high_s, high_r, s).start()
+
+    @pl.loop(0, need_ref.shape[0] // GROUPS)
+    def _(c):
+        columns = columns_of(need_ref, c * GROUPS)
+        rows = span(c, ROWS)
+        col_need[rows, :] = jnp.concatenate(columns, axis=0)
+        reply_ref[rows, :] = gathered(pick(columns, half), columns, half, node2[...]).astype(BF)
+
+    @pl.loop(1, n_dom)
+    def _(s):
+        reply(s).start()
+
+    got_ref[span(dom, CAP), :] = reply_ref[span(dom, CAP), :]
+    halo_up.wait_recv()
+    halo_down.wait_recv()
+    ext2[:HALO, :D] = before_ref[...]
+    ext2[half:, D:] = after_ref[...]
+    lat_in.wait()
+
+
+    @pl.loop(0, steps)
+    def _(c):
+        rows = span(c, ROWS)
+        columns = columns_of(src_ref, c * GROUPS)
+        col_src[rows, :] = jnp.concatenate(columns, axis=0)
+        source = gathered(pick(columns, wide), columns, wide, ext2[...]).astype(BF)
+        source_ref[rows, :] = source
+        lat = lat_ref[rows, :]
+        inputs = jnp.concatenate([lat, source, target_ref[rows, :]], axis=1)
+        pre_one = nn(inputs, first_ref[0]) + bias_ref[0, 0:1, :]
+        _, _, pre_two, _, _, centred, inv_std = layers(0, pre_one, rest_ref, bias_ref)
+        message = centred * inv_std * gain_ref[0:1, :] + bias_ref[0, 3:4, :]
+        new_ref[rows, :] = (lat.astype(F32) + message).astype(BF)
+        new_out(c).start()
+        one_ref[rows, :] = pre_one
+        two_ref[rows, :] = pre_two
+        centred_ref[rows, :] = centred
+        spot = put(dst_ref, c * GROUPS, half)
+        put_dst[c] = spot
+        acc_dst[...] += nn(spot, halved(message, load_columns(col_dst, c * ROWS), half))
+
+    @pl.loop(1, n_dom)
+    def _(s):
+        reply(s).wait_recv()
+
+
+    got2[:, :D] = got_ref[:slots, :]
+    got2[:, D:] = got_ref[slots:, :]
+    live_rows = count_ref[0]
+    keep = (lax.broadcasted_iota(jnp.int32, (512, D), 0) < live_rows).astype(F32)
+    slot_columns = columns_of(slot_ref, 0)
+    world_columns = columns_of(wdst_ref, 0)
+    world_pick = pick(world_columns, half)
+    world_put = put(wdst_ref, 0, half)
+    lat = wlat_ref[...]
+    inputs = jnp.concatenate(
+        [
+            lat,
+            gathered(pick(slot_columns, slots), slot_columns, slots, got2[...]).astype(BF),
+            gathered(world_pick, world_columns, half, node2[...]).astype(BF),
+        ],
+        axis=1,
+    )
+    pre_one = nn(inputs, first_ref[1]) + bias_ref[1, 0:1, :]
+    sig_one, act_one, pre_two, sig_two, act_two, centred, inv_std = layers(
+        1, pre_one, rest_ref, bias_ref
+    )
+    normed = centred * inv_std
+    message = keep * (normed * gain_ref[1:2, :] + bias_ref[1, 3:4, :])
+    new_world_ref[...] = (lat.astype(F32) + message).astype(BF)
+    world_sum = nn(world_put, halved(message, world_columns, half)).astype(BF)
+
+    for h in range(2):
+        rows = slice(h * half, h * half + half)
+        side = slice(h * D, h * D + D)
+        node = node_ref[rows, :]
+        n_inputs = jnp.concatenate([node, acc_dst[:, side].astype(BF), world_sum[:, side]], axis=1)
+        n_one = nn(n_inputs, first_ref[2]) + bias_ref[2, 0:1, :]
+        n_sig_one, n_act_one, n_two, n_sig_two, n_act_two, n_centred, n_inv = layers(
+            2, n_one, rest_ref, bias_ref
+        )
+        n_normed = n_centred * n_inv
+        new_nodes_ref[rows, :] = (
+            node.astype(F32) + n_normed * gain_ref[2:3, :] + bias_ref[2, 3:4, :]
+        ).astype(BF)
+        n_cot = node_cot_ref[rows, :].astype(F32)
+        e_one, e_two, e_three, sums = layers_back(
+            2, n_cot, n_one, n_sig_one, n_two, n_sig_two, n_normed, n_inv, rest_ref, gain_ref
+        )
+        if h == 0:
+            weight_ref[: 3 * D, :] = tn(n_inputs, e_one)
+            weight_ref[3 * D : 4 * D, :] = tn(n_act_one, e_two)
+            weight_ref[4 * D :, :] = tn(n_act_two, e_three)
+            sums_ref[...] = sums
+        else:
+            weight_ref[: 3 * D, :] += tn(n_inputs, e_one)
+            weight_ref[3 * D : 4 * D, :] += tn(n_act_one, e_two)
+            weight_ref[4 * D :, :] += tn(n_act_two, e_three)
+            sums_ref[...] += sums
+        part2[:, side] = n_cot + nt(e_one, first_ref[2, :D, :])
+        back2[:, side] = nt(e_one, first_ref[2, D : 2 * D, :]).astype(BF)
+        world_back2[:, side] = nt(e_one, first_ref[2, 2 * D :, :]).astype(BF)
+
+    own_cot = wcot_ref[...].astype(F32)
+    cot = keep * (own_cot + gathered(world_pick, world_columns, half, world_back2[...]))
+    d_one, d_two, d_three, sums = layers_back(
+        1, cot, pre_one, sig_one, pre_two, sig_two, normed, inv_std, rest_ref, gain_ref
+    )
+    to_source = nt(d_one, first_ref[1, D : 2 * D, :])
+    placed = nn(put(slot_ref, 0, slots), halved(to_source, slot_columns, slots)).astype(BF)
+    sent_ref[:slots, :] = placed[:, :D]
+    sent_ref[slots:, :] = placed[:, D:]
+
+    early[: 3 * D, :] = tn(inputs, d_one).astype(BF)
+    early[3 * D : 4 * D, :] = tn(act_one, d_two).astype(BF)
+    early[4 * D : 640, :] = tn(act_two, d_three).astype(BF)
+    early[640:1280, :] = weight_ref[...].astype(BF)
+    tiny_ref[:8, :] = sums
+    tiny_ref[8:, :] = sums_ref[...]
+    for s in range(1, n_dp):
+        quarter(s).start()
+
+    @pl.loop(1, n_dom)
+    def _(s):
+        give_back(s).start()
+
+    returned_ref[span(dom, CAP), :] = sent_ref[span(dom, CAP), :]
+    grad_world_ref[...] = (own_cot + nt(d_one, first_ref[1, :D, :])).astype(BF)
+    to_target = nt(d_one, first_ref[1, 2 * D :, :])
+    part2[...] += nn(world_put, halved(to_target, world_columns, half))
+
+
+    weight_ref[...] = jnp.zeros(weight_ref.shape, F32)
+    sums_ref[...] = jnp.zeros(sums_ref.shape, F32)
+    acc_dst[...] = jnp.zeros(acc_dst.shape, F32)
+    acc_src[...] = jnp.zeros(acc_src.shape, F32)
+    cot_in.wait()
+
+    def chunk(c, carry):
+        rows = span(c, ROWS)
+        own = cot_ref[rows, :].astype(F32)
+        columns = load_columns(col_dst, c * ROWS)
+        cot = own + gathered(pick_dst[rows, :], columns, half, back2[...])
+        pre_one = one_ref[rows, :]
+        pre_two = two_ref[rows, :]
+        centred = centred_ref[rows, :]
+        sig_one = sigma(pre_one)
+        sig_two = sigma(pre_two)
+        inv_std = lax.rsqrt(lane_mean(centred * centred) + EPS)
+        normed = centred * inv_std
+        d_one, d_two, d_three, sums = layers_back(
+            0, cot, pre_one, sig_one, pre_two, sig_two, normed, inv_std, rest_ref, gain_ref
+        )
+        d_ref[rows, :] = d_one
+        grad_ref[rows, :] = (own + nt(d_one, first_ref[0, :D, :])).astype(BF)
+        grad_out(c).start()
+        weight_ref[:D, :] += tn(lat_ref[rows, :], d_one)
+        weight_ref[D : 2 * D, :] += tn(source_ref[rows, :], d_one)
+        weight_ref[2 * D : 3 * D, :] += tn(target_ref[rows, :], d_one)
+        weight_ref[3 * D : 4 * D, :] += tn((pre_one * sig_one).astype(BF), d_two)
+        weight_ref[4 * D :, :] += tn((pre_two * sig_two).astype(BF), d_three)
+        sums_ref[...] += sums
+        return carry
+
+    n_early = QUARTER // EARLY
+    lax.fori_loop(0, steps // 3, chunk, 0)
+
+    total = early[span(dp, QUARTER), :].astype(F32)
+    for s in range(1, n_dp):
+        quarter(s).wait_recv()
+        total = total + early_got[span(lax.rem(dp - s + n_dp, n_dp), QUARTER), :].astype(F32)
+    early_mid[...] = total
+
+    @pl.loop(1, n_dom)
+    def _(s):
+        @pl.when(lax.rem(dom + s, n_dom) < n_early)
+        def _():
+            middle(s).start()
+
+    lax.fori_loop(steps // 3, 2 * steps // 3, chunk, 0)
+
+    @pl.when(dom < n_early)
+    def _():
+        total = collected(EARLY, early_mid, early_mid_got, b_s, b_r)
+        early_out[mine(), :] = (total * scale).astype(BF)
+
+        @pl.loop(1, n_dom)
+        def _(s):
+            ready(s).start()
+
+    lax.fori_loop(2 * steps // 3, steps, chunk, 0)
+
+    late[:640, :] = weight_ref[...].astype(BF)
+    late[640:, :] = jnp.concatenate(
+        [sums_ref[...], tiny_ref[...], jnp.zeros((N_LATE - 664, D), F32)], axis=0
+    ).astype(BF)
+    n_late = N_LATE // LATE
+
+    @pl.loop(1, n_dom)
+    def _(s):
+        @pl.when(lax.rem(dom + s, n_dom) < n_late)
+        def _():
+            scatter(LATE, late, late_got, d_s, d_r, s).start()
+
+    @pl.loop(1, n_dom)
+    def _(s):
+        @pl.when(lax.rem(dom - s + n_dom, n_dom) < n_early)
+        def _():
+            ready(s).wait_recv()
+
+    for s in range(1, n_dp):
+        quarters(s).start()
+
+
+    @pl.loop(0, steps)
+    def _(c):
+        columns = load_columns(col_src, c * ROWS)
+        values = d_ref[span(c, ROWS), :].astype(F32)
+        acc_src[...] += nn(put(src_ref, c * GROUPS, wide), halved(values, columns, wide))
+
+    weight_src = first_ref[0, D : 2 * D, :]
+    left_ref[...] = nt(acc_src[:HALO, :D].astype(BF), weight_src).astype(BF)
+    right_ref[...] = nt(acc_src[half:, D:].astype(BF), weight_src).astype(BF)
+    rim_down = neighbour(left_ref, from_right_ref, rim_s, rim_r, 0, n_dom - 1)
+    rim_up = neighbour(right_ref, from_left_ref, rim_s, rim_r, 1, 1)
+    rim_down.start()
+    rim_up.start()
+
+    @pl.when(dom < n_late)
+    def _():
+        late_pair[dp] = collected(LATE, late, late_got, d_s, d_r)
+        for s in range(1, n_dp):
+            swap(late_pair, e_s, e_r, s).start()
+
+    @pl.loop(0, steps)
+    def _(c):
+        columns = load_columns(col_dst, c * ROWS)
+        values = d_ref[span(c, ROWS), :].astype(F32)
+        acc_dst[...] += nn(put_dst[c], halved(values, columns, half))
+
+    @pl.when(dom < n_late)
+    def _():
+        late_out[span(dom, LATE), :] = paired(late_pair, e_s, e_r)
+
+        @pl.loop(1, n_dom)
+        def _(s):
+            spread(LATE, late_out, f_s, f_r, s).start()
+
+    for h in range(2):
+        side = slice(h * D, h * D + D)
+        inner = acc_src[HALO:, :D] if h == 0 else acc_src[:half, D:]
+        part2[:, side] += nt(inner.astype(BF), weight_src) + nt(
+            acc_dst[:, side].astype(BF), first_ref[0, 2 * D :, :]
+        )
+
+    @pl.loop(1, n_dom)
+    def _(s):
+        give_back(s).wait_recv()
+
+    @pl.loop(0, need_ref.shape[0] // GROUPS)
+    def _(c):
+        columns = load_columns(col_need, c * ROWS)
+        values = returned_ref[span(c, ROWS), :].astype(F32)
+        part2[...] += nn(put(need_ref, c * GROUPS, half), halved(values, columns, half))
+
+    rim_down.wait()
+    rim_up.wait()
+    part2[:HALO, :D] += from_left_ref[...].astype(F32)
+    part2[half - HALO :, D:] += from_right_ref[...].astype(F32)
+    grad_nodes_ref[:half, :] = part2[:, :D].astype(BF)
+    grad_nodes_ref[half:, :] = part2[:, D:].astype(BF)
+
+    for s in range(1, n_dp):
+        swap(high_ref, high_s, high_r, s).wait()
+        quarter(s).wait_send()
+        quarters(s).wait()
+    high = high_ref[0]
+    for i in range(1, n_dp):
+        high = jnp.maximum(high, high_ref[i])
+    most_ref[0] = jnp.max(high)
+    halo_up.wait_send()
+    halo_down.wait_send()
+
+    @pl.loop(0, steps)
+    def _(c):
+        new_out(c).wait()
+        grad_out(c).wait()
+
+    @pl.loop(1, n_dom)
+    def _(s):
+        ask(s).wait_send()
+        reply(s).wait_send()
+        give_back(s).wait_send()
+
+        @pl.when(lax.rem(dom + s, n_dom) < n_early)
+        def _():
+            middle(s).wait_send()
+
+        @pl.when(dom < n_early)
+        def _():
+            ready(s).wait_send()
+
+        @pl.when(lax.rem(dom + s, n_dom) < n_late)
+        def _():
+            scatter(LATE, late, late_got, d_s, d_r, s).wait_send()
+
+        @pl.when(dom < n_late)
+        def _():
+            spread(LATE, late_out, f_s, f_r, s).wait_send()
+
+        @pl.when(lax.rem(dom - s + n_dom, n_dom) < n_late)
+        def _():
+            spread(LATE, late_out, f_s, f_r, s).wait_recv()
+
+    @pl.when(dom < n_late)
+    def _():
+        for s in range(1, n_dp):
+            swap(late_pair, e_s, e_r, s).wait_send()
+
+
+def finish_kernel(*refs):
+    sources, targets, held = refs[:8], refs[8:18], refs[18:30]
+    in_s, out_s = refs[30:]
+    early_ref, late_ref = held[:2]
+    weights = held[8:]
+    first_ref, rest_ref, bias_ref, gain_ref = weights
+    taken = [pltpu.make_async_copy(sources[i], held[i], in_s.at[i]) for i in range(8)]
+    given = [
+        pltpu.make_async_copy(from_ref, targets[i], out_s.at[i])
+        for i, from_ref in enumerate(list(held[2:8]) + list(weights))
+    ]
+    for copy in taken:
+        copy.start()
+    taken[0].wait()
+    taken[1].wait()
+    small = late_ref[640:672, :].astype(F32)
+    for k, (ref, at) in enumerate(((late_ref, 0), (early_ref, 0), (early_ref, 640))):
+        first_ref[k] = ref[at : at + 384, :].astype(F32)
+        rest_ref[k, 0] = ref[at + 384 : at + 512, :].astype(F32)
+        rest_ref[k, 1] = ref[at + 512 : at + 640, :].astype(F32)
+        bias_ref[k] = small[8 * k : 8 * k + 4, :]
+        gain_ref[k : k + 1, :] = small[8 * k + 4 : 8 * k + 5, :]
+    for i in range(6, 10):
+        given[i].start()
+    for came, go in zip(taken[2:], given):
+        came.wait()
+        go.start()
+    for copy in given:
+        copy.wait()
+
+
+VMEM = pl.BlockSpec(memory_space=pltpu.VMEM)
+SMEM = pl.BlockSpec(memory_space=pltpu.SMEM)
+ANY = pl.BlockSpec(memory_space=pl.ANY)
+
+
+def shape(rows, dtype):
+    return jax.ShapeDtypeStruct((rows, D), dtype)
+
+
+def per_device(
+    node_latents,
+    mesh_latents,
+    world_latents,
+    mesh_src,
+    mesh_dst,
+    world_src,
+    world_dst,
+    send_blocks,
+    world_count,
+    node_cot,
+    mesh_cot,
+    world_cot,
+    first_weights,
+    rest_weights,
+    biases,
+    gains,
+):
+    n_dom = lax.axis_size("dom")
+    n_dp = lax.axis_size("dp")
+    n_mesh = mesh_latents.shape[0]
+    n_world = world_latents.shape[0]
+    steps = n_mesh // ROWS
+    half = NODES // 2
+    slots = n_dom * CAP
+    n_early = n_dp * QUARTER
+
+    def vm(rows, dtype, width=D):
+        return pltpu.VMEM((rows, width), dtype)
+
+    def dma(*count):
+        return pltpu.SemaphoreType.DMA(count)
+
+    def tiles(count):
+        return pltpu.VMEM((count, 8, 128), jnp.int32)
+
+    (
+        new_nodes, new_world, grad_nodes, grad_world, early, late, most, new_mesh, grad_mesh
+    ) = pl.pallas_call(
+        functools.partial(cloth_kernel, n_dom, n_dp),
+        out_shape=[
+            shape(NODES, BF), shape(n_world, BF), shape(NODES, BF), shape(n_world, BF),
+            shape(n_early, BF), shape(N_LATE, BF), jax.ShapeDtypeStruct((1,), jnp.int32),
+            shape(n_mesh, BF), shape(n_mesh, BF),
+        ],
+        in_specs=[SMEM] + [VMEM] * 13 + [ANY] * 2,
+        out_specs=[VMEM] * 6 + [SMEM] + [ANY] * 2,
+        scratch_shapes=[
+            vm(n_mesh, BF), vm(n_mesh, BF), vm(n_mesh, BF), vm(n_mesh, BF),
+            vm(n_mesh, BF), vm(n_mesh, BF),
+            vm(n_mesh, F32), vm(n_mesh, F32), vm(n_mesh, F32), vm(n_mesh, BF),
+            vm(n_mesh, jnp.int32), vm(n_mesh, jnp.int32), vm(slots, jnp.int32),
+            vm(n_mesh, BF, half), pltpu.VMEM((steps, half, ROWS), BF),
+            vm(half, BF, 2 * D), vm(768, BF, 2 * D),
+            vm(half, BF, 2 * D), vm(half, BF, 2 * D),
+            vm(slots, BF), vm(slots // 2, BF, 2 * D),
+            vm(HALO, BF), vm(HALO, BF),
+            pltpu.VMEM((4, 128), jnp.int32), pltpu.VMEM((slots // 128, 128), jnp.int32),
+            tiles(n_dom), tiles(n_dom), vm(slots, BF), tiles(n_dp),
+            vm(half, F32, 2 * D), vm(768, F32, 2 * D), vm(half, F32, 2 * D),
+            vm(640, F32), vm(8, F32),
+            vm(slots, BF), vm(slots, BF),
+            vm(HALO, BF), vm(HALO, BF), vm(HALO, BF), vm(HALO, BF),
+            vm(n_early, BF), vm(n_early, BF), vm(QUARTER, F32), vm(n_dom * EARLY, F32),
+            vm(16, F32),
+            vm(N_LATE, BF), vm(n_dom * LATE, BF), pltpu.VMEM((n_dp, LATE, D), F32),
+            dma(2), dma(2, steps),
+            dma(n_dom), dma(n_dom), dma(n_dom), dma(n_dom), dma(2), dma(2), dma(n_dp), dma(n_dp),
+            dma(n_dom), dma(n_dom), dma(2), dma(2),
+            dma(n_dp), dma(n_dp), dma(n_dom), dma(n_dom), dma(n_dom), dma(n_dom),
+            dma(n_dom), dma(n_dom), dma(n_dp), dma(n_dp), dma(n_dom), dma(n_dom),
+            dma(n_dp), dma(n_dp),
+        ],
+        compiler_params=pltpu.CompilerParams(
+            collective_id=0, has_side_effects=True, vmem_limit_bytes=58 * 1024 * 1024
+        ),
+        name="cloth",
+    )(
+        world_count, world_src.reshape(-1, 128), world_dst.reshape(-1, 128), jnp.transpose(send_blocks[0]),
+        mesh_src.reshape(-1, 128), mesh_dst.reshape(-1, 128), node_latents, node_cot,
+        world_latents, world_cot, first_weights, rest_weights, biases, gains, mesh_latents,
+        mesh_cot,
+    )
+
+    def finish():
+        arrived = [early, late, new_nodes, new_mesh, new_world, grad_nodes, grad_mesh, grad_world]
+        held = [jax.ShapeDtypeStruct(each.shape, each.dtype) for each in arrived]
+        weights = [
+            jax.ShapeDtypeStruct((3, 3 * D, D), F32),
+            jax.ShapeDtypeStruct((3, 2, D, D), F32),
+            jax.ShapeDtypeStruct((3, 4, D), F32),
+            jax.ShapeDtypeStruct((3, D), F32),
+        ]
+        return tuple(
+            pl.pallas_call(
+                finish_kernel,
+                out_shape=held[2:] + weights,
+                in_specs=[ANY] * 8,
+                out_specs=[ANY] * 10,
+                scratch_shapes=[pltpu.VMEM(each.shape, each.dtype) for each in held + weights]
+                + [dma(8), dma(10)],
+                name="finish",
+            )(*arrived)
+        )
+
+    def start_over():
+        return full_exchange(
+            node_latents, mesh_latents, world_latents, mesh_src, mesh_dst, world_src, world_dst,
+            send_blocks, world_count, node_cot, mesh_cot, world_cot, first_weights, rest_weights,
+            biases, gains,
+        )
+
+    return lax.cond(most[0] > CAP, start_over, finish)
 
 
 def solution(mesh):
+    part = P(("dom", "dp"))
+    rows = P(("dom", "dp"), None)
     return jax.shard_map(
         per_device,
         mesh=mesh,
         in_specs=(
-            P(("dom", "dp"), None),
-            P(("dom", "dp"), None),
-            P(("dom", "dp"), None),
-            P(("dom", "dp")),
-            P(("dom", "dp")),
-            P(("dom", "dp")),
-            P(("dom", "dp")),
-            P(("dom", "dp"), None, None),
-            P(("dom", "dp")),
-            P(("dom", "dp"), None),
-            P(("dom", "dp"), None),
-            P(("dom", "dp"), None),
-            P(),
-            P(),
-            P(),
-            P(),
+            rows, rows, rows, part, part, part, part, P(("dom", "dp"), None, None), part, rows,
+            rows, rows, P(), P(), P(), P(),
         ),
-        out_specs=(
-            P(("dom", "dp"), None),
-            P(("dom", "dp"), None),
-            P(("dom", "dp"), None),
-            P(("dom", "dp"), None),
-            P(("dom", "dp"), None),
-            P(("dom", "dp"), None),
-            P(),
-            P(),
-            P(),
-            P(),
-        ),
+        out_specs=(rows, rows, rows, rows, rows, rows, P(), P(), P(), P()),
         check_vma=False,
     )

time: 455 us -> 75.9 us (0.17); the launches traced: 447 us -> 75.8 us
  other arithmetic: 136 us -> 0 us
  local copies, waits for them, and re-layouts: 101 us -> 0.9 us
  Pallas kernels: 0 us -> 72.3 us
  blocking collectives: 67.1 us -> 0 us
  waiting for transfers between devices: 60.6 us -> 0 us
  matrix products: 37.3 us -> 0 us
  starting transfers between devices: 28.1 us -> 0 us
  between operations: 16.5 us -> 2.24 us
    scatter-add x7 -> x0, other arithmetic: 107 us -> none  [the longest x1 44.8 us: per_device(): jax.ops.segment_sum(returned, send_index, num_segments=node_count)]
    gather x9 -> x0, local copies, waits for them, and re-layouts: 72.8 us -> none  [the longest x1 29.5 us: per_device(): node_latents[send_index]]
    pallas_call x0 -> x2, Pallas kernels: none -> 72.3 us  [the longest x1 69.5 us: per_device(): pl.pallas_call(functools.partial(cloth_kernel, n_dom, n_dp), out_shape=[s...]
    psum x1 -> x0, blocking collectives: 67.1 us -> none  [per_device(): lax.psum((jnp.stack([mesh_grads[0], weight_grads[0], node_grads[0]]), jnp...]
    psum x1 -> x0, waiting for transfers between devices: 50 us -> none  [per_device(): lax.psum((jnp.stack([mesh_grads[0], weight_grads[0], node_grads[0]]), jnp...]
    dot_general x27 -> x0, matrix products: 37.3 us -> none  [the longest x9 16.3 us: matmul_nt(): lax.dot_general(left, right, (((1,), (1,)), ((), ())), preferred_element_...]
    unnamed x194 -> x22, local copies, waits for them, and re-layouts: 18.2 us -> 0.9 us
    all_to_all x2 -> x0, starting transfers between devices: 16.2 us -> none  [the longest x1 8.75 us: per_device(): lax.all_to_all(node_latents[send_index], 'dom', split_axis=0, concat_axis...]
  transfers between devices with their start and end apart: 7 -> 0, of which waited for: 3 -> 0; matrix products, arithmetic and copies ran while one was open for 29% -> 0% of each run, Pallas kernels for 0% -> 0%
where the time goes in v2:
time: 75.9 us; the launch traced here: 75.8 us
  Pallas kernels  72.3 us (95%)
  between operations  2.24 us (3%)
  local copies, waits for them, and re-layouts  0.9 us (1%)
    pallas_call x1, Pallas kernels, per_device(): pl.pallas_call(functools.partial(cloth_kernel, n_dom, n_dp), out_shape=[s...  69.5 us
    pallas_call x1, Pallas kernels, finish(): pl.pallas_call(finish_kernel, out_shape=held[2:] + weights, in_specs=[ANY...  2.82 us

profile of v2, /device:TPU:1, one launch (start us, length us, event | category | flops | bytes accessed | tf_op | source)
XLA Modules:
  0.0 75.8 jit_solution(18275002033815026115)
XLA Ops:
  0.6 0.0 copy-start.32
  0.7 0.0 copy-start.61
  0.7 0.0 copy-start.70
  0.7 0.0 copy-start.54
  0.7 0.0 copy-start.27
  0.7 0.0 copy-start.7
  0.7 0.0 copy-start
  1.5 69.5 %cloth.1 = (bf16[1024,128]{1,0:T(8,128)(2,1)S(1)}, bf16[512,128]{1,0:T(8,128)(2,1)}, bf16[1024,128]{1,0:T(8,128)(2,1)}, bf16[512,128]{1,0:T(8,128)(2,1)}, bf16[1...) custom-call(s32[1]{0:T(128)S(6)} %copy.156.count_ref, ...), custom_call_target="tpu_custom_call" | custom-call | tf_op jit(solution)/shard_map/cloth/pallas_call | solution.py:1007
  71.7 0.0 copy-done.32
  71.7 0.0 copy-done.61
  71.7 0.0 copy-done.70
  71.7 0.0 copy-done.54
  71.7 0.0 copy-done.27
  71.7 0.0 copy-done.7
  71.7 0.0 copy-done
  71.7 3.1 %conditional.1 = (bf16[1024,128]{1,0:T(8,128)(2,1)S(1)}, f32[3,384,128]{2,1,0:T(8,128)S(1)}, f32[3,2,128,128]{3,2,1,0:T(8,128)}, f32[3,4,128]{2,1,0:T(4,128)S(1)...) conditional(s32[]{:T(128)} %bitcast.73, ...), branch_computations={%region_0.0_spmd, %region_1.37_spmd} | conditional | flops 2325692928 | bytes 307227584 | solution.py:1081
  71.8 2.8 %finish.1 = (bf16[1024,128]{1,0:T(8,128)(2,1)}, bf16[3072,128]{1,0:T(8,128)(2,1)}, bf16[512,128]{1,0:T(8,128)(2,1)}, bf16[1024,128]{1,0:T(8,128)(2,1)S(1)}, bf16...) custom-call(bf16[1280,128]{1,0:T(8,128)(2,1)S(1)} %get-tuple-element, ...), custom_call_target="tpu_custom_call" | custom-call | tf_op jit(solution)/shard_map/cond/branch_0_fun/finish/pallas_call | solution.py:1063
  74.9 0.0 copy-start.102
  74.9 0.0 copy-start.104
  74.9 0.0 copy-start.105
  74.9 0.0 copy-start.106
  74.9 0.8 %copy-done.102 = f32[3,384,128]{2,1,0:T(8,128)} copy-done((f32[3,384,128]{2,1,0:T(8,128)}, f32[3,384,128]{2,1,0:T(8,128)S(1)}, u32[]{:S(2)}) %copy-start.102) | copy-done | bytes 589848
  75.7 0.1 copy-done.104
  75.8 0.0 copy-done.105
  75.8 0.0 copy-done.106
Async XLA Ops:
  0.6 71.0 %copy-start.32 = (bf16[512,128]{1,0:T(8,128)(2,1)S(1)}, bf16[512,128]{1,0:T(8,128)(2,1)}, u32[]{:S(2)}) copy-start(bf16[512,128]{1,0:T(8,128)(2,1)} %wcot_ref.1) | copy-start | bytes 393220
  0.7 71.0 %copy-start.61 = (s32[1,32,16]{1,2,0:T(8,128)S(1)}, s32[1,32,16]{1,2,0:T(8,128)}, u32[]{:S(2)}) copy-start(s32[1,32,16]{1,2,0:T(8,128)} %param.25) | copy-start | bytes 6148
  0.7 71.0 %copy-start.70 = (s32[512]{0:T(512)S(1)}, s32[512]{0:T(512)}, u32[]{:S(2)}) copy-start(s32[512]{0:T(512)} %param.23) | copy-start | bytes 6148
  0.7 71.0 %copy-start.54 = (s32[3072]{0:T(1024)S(1)}, s32[3072]{0:T(1024)}, u32[]{:S(2)}) copy-start(s32[3072]{0:T(1024)} %param.21) | copy-start | bytes 36868
  0.7 71.0 %copy-start.27 = (bf16[512,128]{1,0:T(8,128)(2,1)S(1)}, bf16[512,128]{1,0:T(8,128)(2,1)}, u32[]{:S(2)}) copy-start(bf16[512,128]{1,0:T(8,128)(2,1)} %wlat_ref.1) | copy-start | bytes 393220
  0.7 71.0 %copy-start.7 = (bf16[3072,128]{1,0:T(8,128)(2,1)S(1)}, bf16[3072,128]{1,0:T(8,128)(2,1)}, u32[]{:S(2)}) copy-start(bf16[3072,128]{1,0:T(8,128)(2,1)} %lat_hbm.1) | copy-start | bytes 2359300
  0.7 71.0 %copy-start = (bf16[1024,128]{1,0:T(8,128)(2,1)S(1)}, bf16[1024,128]{1,0:T(8,128)(2,1)}, u32[]{:S(2)}) copy-start(bf16[1024,128]{1,0:T(8,128)(2,1)} %node_ref.1) | copy-start | bytes 786436
  74.9 0.8 %copy-start.102 = (f32[3,384,128]{2,1,0:T(8,128)}, f32[3,384,128]{2,1,0:T(8,128)S(1)}, u32[]{:S(2)}) copy-start(f32[3,384,128]{2,1,0:T(8,128)S(1)} %get-tuple-element.188) | copy-start | bytes 1769476
  74.9 0.9 %copy-start.104 = (bf16[1024,128]{1,0:T(8,128)(2,1)}, bf16[1024,128]{1,0:T(8,128)(2,1)S(1)}, u32[]{:S(2)}) copy-start(bf16[1024,128]{1,0:T(8,128)(2,1)S(1)} %get-tuple-element.185) | copy-start | bytes 786436
  74.9 0.9 %copy-start.105 = (f32[3,4,128]{2,1,0:T(4,128)}, f32[3,4,128]{2,1,0:T(4,128)S(1)}, u32[]{:S(2)}) copy-start(f32[3,4,128]{2,1,0:T(4,128)S(1)} %get-tuple-element.190) | copy-start | bytes 18436
  74.9 0.9 %copy-start.106 = (f32[3,128]{1,0:T(4,128)}, f32[3,128]{1,0:T(4,128)S(1)}, u32[]{:S(2)}) copy-start(f32[3,128]{1,0:T(4,128)S(1)} %get-tuple-element.191) | copy-start | bytes 4612

commit v3 on v2

--- a/solution.py
+++ b/solution.py
@@ -457,7 +457,7 @@
     new_mesh_hbm, grad_mesh_hbm, lat_ref, cot_ref, new_ref, grad_ref, source_ref, target_ref,
     one_ref, two_ref, centred_ref, d_ref, col_src, col_dst, col_need, pick_dst, put_dst, node2,
     ext2, back2, world_back2, got_ref, got2, before_ref, after_ref, slot_ref, need_ref, ask_ref,
-    asked_ref, reply_ref, high_ref, acc_dst, acc_src, part2, weight_ref, sums_ref, sent_ref,
+    asked_ref, reply_ref, high_ref, acc_dst, acc_src, part2, weight_ref, first_t, sums_ref, sent_ref,
     returned_ref, left_ref, right_ref, from_left_ref, from_right_ref, early, early_got, early_mid,
     early_mid_got, tiny_ref, late, late_got, late_pair, in_s, out_s, ask_s, ask_r, reply_s, reply_r, halo_s, halo_r, high_s,
     high_r, back_s, back_r, rim_s, rim_r, a_s, a_r, b_s, b_r, c_s, c_r, d_s,
@@ -577,12 +577,13 @@
     halo_down = neighbour(node_ref.at[pl.ds(0, HALO)], after_ref, halo_s, halo_r, 1, n_dom - 1)
 
 
+    halo_up.start()
+    halo_down.start()
+
     @pl.loop(1, n_dom)
     def _(s):
         ask(s).start()
 
-    halo_up.start()
-    halo_down.start()
     asked_ref[dom] = ask_ref[dom]
     node2[:, :D] = node_ref[:half, :]
     node2[:, D:] = node_ref[half:, :]
@@ -599,26 +600,6 @@
         pick_dst[rows, :] = picked
         target_ref[rows, :] = gathered(picked, columns, half, node2[...]).astype(BF)
 
-    @pl.loop(1, n_dom)
-    def _(s):
-        ask(s).wait_recv()
-
-    high_ref[dp] = jnp.broadcast_to(asked_rows(asked_ref, blocks_ref, need_ref), (8, 128))
-    for s in range(1, n_dp):
-        swap(high_ref, high_s, high_r, s).start()
-
-    @pl.loop(0, need_ref.shape[0] // GROUPS)
-    def _(c):
-        columns = columns_of(need_ref, c * GROUPS)
-        rows = span(c, ROWS)
-        col_need[rows, :] = jnp.concatenate(columns, axis=0)
-        reply_ref[rows, :] = gathered(pick(columns, half), columns, half, node2[...]).astype(BF)
-
-    @pl.loop(1, n_dom)
-    def _(s):
-        reply(s).start()
-
-    got_ref[span(dom, CAP), :] = reply_ref[span(dom, CAP), :]
     halo_up.wait_recv()
     halo_down.wait_recv()
     ext2[:HALO, :D] = before_ref[...]
@@ -626,8 +607,7 @@
     lat_in.wait()
 
 
-    @pl.loop(0, steps)
-    def _(c):
+    def ahead(c, carry):
         rows = span(c, ROWS)
         columns = columns_of(src_ref, c * GROUPS)
         col_src[rows, :] = jnp.concatenate(columns, axis=0)
@@ -646,6 +626,31 @@
         spot = put(dst_ref, c * GROUPS, half)
         put_dst[c] = spot
         acc_dst[...] += nn(spot, halved(message, load_columns(col_dst, c * ROWS), half))
+        return carry
+
+    lax.fori_loop(0, 1, ahead, 0)
+
+    @pl.loop(1, n_dom)
+    def _(s):
+        ask(s).wait_recv()
+
+    high_ref[dp] = jnp.broadcast_to(asked_rows(asked_ref, blocks_ref, need_ref), (8, 128))
+    for s in range(1, n_dp):
+        swap(high_ref, high_s, high_r, s).start()
+
+    @pl.loop(0, need_ref.shape[0] // GROUPS)
+    def _(c):
+        columns = columns_of(need_ref, c * GROUPS)
+        rows = span(c, ROWS)
+        col_need[rows, :] = jnp.concatenate(columns, axis=0)
+        reply_ref[rows, :] = gathered(pick(columns, half), columns, half, node2[...]).astype(BF)
+
+    @pl.loop(1, n_dom)
+    def _(s):
+        reply(s).start()
+
+    got_ref[span(dom, CAP), :] = reply_ref[span(dom, CAP), :]
+    lax.fori_loop(1, steps, ahead, 0)
 
     @pl.loop(1, n_dom)
     def _(s):
@@ -739,6 +744,7 @@
 
 
     weight_ref[...] = jnp.zeros(weight_ref.shape, F32)
+    first_t[...] = jnp.zeros(first_t.shape, F32)
     sums_ref[...] = jnp.zeros(sums_ref.shape, F32)
     acc_dst[...] = jnp.zeros(acc_dst.shape, F32)
     acc_src[...] = jnp.zeros(acc_src.shape, F32)
@@ -762,16 +768,17 @@
         d_ref[rows, :] = d_one
         grad_ref[rows, :] = (own + nt(d_one, first_ref[0, :D, :])).astype(BF)
         grad_out(c).start()
-        weight_ref[:D, :] += tn(lat_ref[rows, :], d_one)
-        weight_ref[D : 2 * D, :] += tn(source_ref[rows, :], d_one)
-        weight_ref[2 * D : 3 * D, :] += tn(target_ref[rows, :], d_one)
+        inputs = jnp.concatenate(
+            [lat_ref[rows, :], source_ref[rows, :], target_ref[rows, :]], axis=1
+        )
+        first_t[...] += tn(d_one, inputs)
         weight_ref[3 * D : 4 * D, :] += tn((pre_one * sig_one).astype(BF), d_two)
         weight_ref[4 * D :, :] += tn((pre_two * sig_two).astype(BF), d_three)
         sums_ref[...] += sums
         return carry
 
     n_early = QUARTER // EARLY
-    lax.fori_loop(0, steps // 3, chunk, 0)
+    lax.fori_loop(0, steps // 2, chunk, 0)
 
     total = early[span(dp, QUARTER), :].astype(F32)
     for s in range(1, n_dp):
@@ -785,20 +792,11 @@
         def _():
             middle(s).start()
 
-    lax.fori_loop(steps // 3, 2 * steps // 3, chunk, 0)
-
-    @pl.when(dom < n_early)
-    def _():
-        total = collected(EARLY, early_mid, early_mid_got, b_s, b_r)
-        early_out[mine(), :] = (total * scale).astype(BF)
-
-        @pl.loop(1, n_dom)
-        def _(s):
-            ready(s).start()
-
-    lax.fori_loop(2 * steps // 3, steps, chunk, 0)
-
-    late[:640, :] = weight_ref[...].astype(BF)
+    lax.fori_loop(steps // 2, steps, chunk, 0)
+
+    for k in range(3):
+        late[k * D : (k + 1) * D, :] = jnp.transpose(first_t[:, k * D : (k + 1) * D]).astype(BF)
+    late[3 * D : 640, :] = weight_ref[3 * D :, :].astype(BF)
     late[640:, :] = jnp.concatenate(
         [sums_ref[...], tiny_ref[...], jnp.zeros((N_LATE - 664, D), F32)], axis=0
     ).astype(BF)
@@ -810,14 +808,14 @@
         def _():
             scatter(LATE, late, late_got, d_s, d_r, s).start()
 
-    @pl.loop(1, n_dom)
-    def _(s):
-        @pl.when(lax.rem(dom - s + n_dom, n_dom) < n_early)
-        def _():
-            ready(s).wait_recv()
-
-    for s in range(1, n_dp):
-        quarters(s).start()
+    @pl.when(dom < n_early)
+    def _():
+        total = collected(EARLY, early_mid, early_mid_got, b_s, b_r)
+        early_out[mine(), :] = (total * scale).astype(BF)
+
+        @pl.loop(1, n_dom)
+        def _(s):
+            ready(s).start()
 
 
     @pl.loop(0, steps)
@@ -839,6 +837,15 @@
         late_pair[dp] = collected(LATE, late, late_got, d_s, d_r)
         for s in range(1, n_dp):
             swap(late_pair, e_s, e_r, s).start()
+
+    @pl.loop(1, n_dom)
+    def _(s):
+        @pl.when(lax.rem(dom - s + n_dom, n_dom) < n_early)
+        def _():
+            ready(s).wait_recv()
+
+    for s in range(1, n_dp):
+        quarters(s).start()
 
     @pl.loop(0, steps)
     def _(c):
@@ -1026,7 +1033,7 @@
             pltpu.VMEM((4, 128), jnp.int32), pltpu.VMEM((slots // 128, 128), jnp.int32),
             tiles(n_dom), tiles(n_dom), vm(slots, BF), tiles(n_dp),
             vm(half, F32, 2 * D), vm(768, F32, 2 * D), vm(half, F32, 2 * D),
-            vm(640, F32), vm(8, F32),
+            vm(640, F32), vm(D, F32, 3 * D), vm(8, F32),
             vm(slots, BF), vm(slots, BF),
             vm(HALO, BF), vm(HALO, BF), vm(HALO, BF), vm(HALO, BF),
             vm(n_early, BF), vm(n_early, BF), vm(QUARTER, F32), vm(n_dom * EARLY, F32),

time: 75.9 us -> 70.9 us (0.934)
  Pallas kernels: 72.3 us -> 67.3 us
    pallas_call x1, Pallas kernels: 69.5 us -> 64.5 us  [per_device(): pl.pallas_call(functools.partial(cloth_kernel, n_dom, n_dp), out_shape=[s...]
where the time goes in v3:
time: 70.9 us; the launch traced here: 70.7 us
  Pallas kernels  67.3 us (95%)
  between operations  2.24 us (3%)
  local copies, waits for them, and re-layouts  0.9 us (1%)
    pallas_call x1, Pallas kernels, per_device(): pl.pallas_call(functools.partial(cloth_kernel, n_dom, n_dp), out_shape=[s...  64.5 us
    pallas_call x1, Pallas kernels, finish(): pl.pallas_call(finish_kernel, out_shape=held[2:] + weights, in_specs=[ANY...  2.82 us

profile of v3, /device:TPU:1, one launch (start us, length us, event | category | flops | bytes accessed | tf_op | source)
XLA Modules:
  0.0 70.7 jit_solution(13832510059650061915)
XLA Ops:
  0.6 0.0 copy-start.32
  0.7 0.0 copy-start.61
  0.7 0.0 copy-start.70
  0.7 0.0 copy-start.54
  0.7 0.0 copy-start.27
  0.7 0.0 copy-start.7
  0.7 0.0 copy-start
  1.5 64.5 %cloth.1 = (bf16[1024,128]{1,0:T(8,128)(2,1)S(1)}, bf16[512,128]{1,0:T(8,128)(2,1)}, bf16[1024,128]{1,0:T(8,128)(2,1)}, bf16[512,128]{1,0:T(8,128)(2,1)}, bf16[1...) custom-call(s32[1]{0:T(128)S(6)} %copy.156.count_ref, ...), custom_call_target="tpu_custom_call" | custom-call | tf_op jit(solution)/shard_map/cloth/pallas_call | solution.py:1014
  66.6 0.0 copy-done.32
  66.6 0.0 copy-done.61
  66.6 0.0 copy-done.70
  66.6 0.0 copy-done.54
  66.7 0.0 copy-done.27
  66.7 0.0 copy-done.7
  66.7 0.0 copy-done
  66.7 3.1 %conditional.1 = (bf16[1024,128]{1,0:T(8,128)(2,1)S(1)}, f32[3,384,128]{2,1,0:T(8,128)S(1)}, f32[3,2,128,128]{3,2,1,0:T(8,128)}, f32[3,4,128]{2,1,0:T(4,128)S(1)...) conditional(s32[]{:T(128)} %bitcast.73, ...), branch_computations={%region_0.0_spmd, %region_1.37_spmd} | conditional | flops 2325692928 | bytes 307227584 | solution.py:1088
  66.7 2.8 %finish.1 = (bf16[1024,128]{1,0:T(8,128)(2,1)}, bf16[3072,128]{1,0:T(8,128)(2,1)}, bf16[512,128]{1,0:T(8,128)(2,1)}, bf16[1024,128]{1,0:T(8,128)(2,1)S(1)}, bf16...) custom-call(bf16[1280,128]{1,0:T(8,128)(2,1)S(1)} %get-tuple-element, ...), custom_call_target="tpu_custom_call" | custom-call | tf_op jit(solution)/shard_map/cond/branch_0_fun/finish/pallas_call | solution.py:1070
  69.8 0.0 copy-start.102
  69.8 0.0 copy-start.104
  69.8 0.0 copy-start.105
  69.8 0.0 copy-start.106
  69.8 0.8 %copy-done.102 = f32[3,384,128]{2,1,0:T(8,128)} copy-done((f32[3,384,128]{2,1,0:T(8,128)}, f32[3,384,128]{2,1,0:T(8,128)S(1)}, u32[]{:S(2)}) %copy-start.102) | copy-done | bytes 589848
  70.6 0.1 copy-done.104
  70.7 0.0 copy-done.105
  70.7 0.0 copy-done.106
Async XLA Ops:
  0.6 66.0 %copy-start.32 = (bf16[512,128]{1,0:T(8,128)(2,1)S(1)}, bf16[512,128]{1,0:T(8,128)(2,1)}, u32[]{:S(2)}) copy-start(bf16[512,128]{1,0:T(8,128)(2,1)} %wcot_ref.1) | copy-start | bytes 393220
  0.7 66.0 %copy-start.61 = (s32[1,32,16]{1,2,0:T(8,128)S(1)}, s32[1,32,16]{1,2,0:T(8,128)}, u32[]{:S(2)}) copy-start(s32[1,32,16]{1,2,0:T(8,128)} %param.25) | copy-start | bytes 6148
  0.7 66.0 %copy-start.70 = (s32[512]{0:T(512)S(1)}, s32[512]{0:T(512)}, u32[]{:S(2)}) copy-start(s32[512]{0:T(512)} %param.23) | copy-start | bytes 6148
  0.7 66.0 %copy-start.54 = (s32[3072]{0:T(1024)S(1)}, s32[3072]{0:T(1024)}, u32[]{:S(2)}) copy-start(s32[3072]{0:T(1024)} %param.21) | copy-start | bytes 36868
  0.7 66.0 %copy-start.27 = (bf16[512,128]{1,0:T(8,128)(2,1)S(1)}, bf16[512,128]{1,0:T(8,128)(2,1)}, u32[]{:S(2)}) copy-start(bf16[512,128]{1,0:T(8,128)(2,1)} %wlat_ref.1) | copy-start | bytes 393220
  0.7 66.0 %copy-start.7 = (bf16[3072,128]{1,0:T(8,128)(2,1)S(1)}, bf16[3072,128]{1,0:T(8,128)(2,1)}, u32[]{:S(2)}) copy-start(bf16[3072,128]{1,0:T(8,128)(2,1)} %lat_hbm.1) | copy-start | bytes 2359300
  0.7 66.0 %copy-start = (bf16[1024,128]{1,0:T(8,128)(2,1)S(1)}, bf16[1024,128]{1,0:T(8,128)(2,1)}, u32[]{:S(2)}) copy-start(bf16[1024,128]{1,0:T(8,128)(2,1)} %node_ref.1) | copy-start | bytes 786436
  69.8 0.8 %copy-start.102 = (f32[3,384,128]{2,1,0:T(8,128)}, f32[3,384,128]{2,1,0:T(8,128)S(1)}, u32[]{:S(2)}) copy-start(f32[3,384,128]{2,1,0:T(8,128)S(1)} %get-tuple-element.188) | copy-start | bytes 1769476
  69.8 0.9 %copy-start.104 = (bf16[1024,128]{1,0:T(8,128)(2,1)}, bf16[1024,128]{1,0:T(8,128)(2,1)S(1)}, u32[]{:S(2)}) copy-start(bf16[1024,128]{1,0:T(8,128)(2,1)S(1)} %get-tuple-element.185) | copy-start | bytes 786436
  69.8 0.9 %copy-start.105 = (f32[3,4,128]{2,1,0:T(4,128)}, f32[3,4,128]{2,1,0:T(4,128)S(1)}, u32[]{:S(2)}) copy-start(f32[3,4,128]{2,1,0:T(4,128)S(1)} %get-tuple-element.190) | copy-start | bytes 18436
  69.8 0.9 %copy-start.106 = (f32[3,128]{1,0:T(4,128)}, f32[3,128]{1,0:T(4,128)S(1)}, u32[]{:S(2)}) copy-start(f32[3,128]{1,0:T(4,128)S(1)} %get-tuple-element.191) | copy-start | bytes 4612
